TPU v7x, 256 devices: a whole 4x4x8 slice. The times are simulated.
256 devices in a mesh: sample: 64 (over z_lo, x, y), depth: 4 (over z_hi, core).
Axes of the slice: x: 4, y: 4, z: 8 (z_hi: 2, z_lo: 4; z = z_hi * 4 + z_lo), core: 2. Of those that a mesh axis runs over, the one named last changes fastest.
Arguments:
- volume: bfloat16 [64, 16, 8, 2048], P('sample', 'depth'), may hold values from -6 to 6
- kernels: bfloat16 [3, 27, 1024], replicated, may hold values from -0.21875 to 0.21875
- partner: int32 [64], replicated, may hold values from 0 to 63, each once
- cotangent: bfloat16 [64, 16, 8, 2048], P('sample', 'depth'), may hold values from -6 to 6
Outputs:
- grad_volume: bfloat16 [64, 16, 8, 2048], P('sample', 'depth')
- kernel_grads: float32 [64, 3, 27, 1024], P('sample')
Inputs may be any that keep to these rules, and one draw needn't show every extreme that they name: partner is a permutation of the 64 crops: every crop is the partner of exactly one crop, and a crop may be its own partner.
All inputs are finite; a program needn't handle non-finite values.
Results may differ from a plain program's by a relative error of at most 0.014.
Values may be sent and summed in bfloat16 or wider, within the bound.
A program may use at most 64 MiB of HBM per device.

v0:
```python
import functools

import jax
import jax.numpy as jnp
from jax import lax
from jax.experimental import pallas as pl
from jax.experimental.pallas import tpu as pltpu
from jax.sharding import PartitionSpec as P

CH = 32
OWN_SHARE = 0.6
PARTNER_SHARE = 0.4
MESH = pl.DeviceIdType.MESH
F32 = jnp.float32
BF16 = jnp.bfloat16
ROWS = 256
LANES = 256
LAYER = 64
NT = (((1,), (1,)), ((), ()))
TN = (((0,), (0,)), ((), ()))


def logistic(v):
    return 0.5 * jnp.tanh(0.5 * v) + 0.5


def block_transpose(y):
    sub = lax.broadcasted_iota(jnp.int32, y.shape, 1) % 4
    blk = lax.broadcasted_iota(jnp.int32, y.shape, 2) // 32
    delta = sub - blk
    turned = [y] + [pltpu.roll(y, 128 - 32 * m, 2) for m in (1, 2, 3)]
    out = y
    for m in (1, 2, 3):
        out = jnp.where(delta == m, pltpu.roll(turned[m], m, 1), out)
        out = jnp.where(delta == m - 4, pltpu.roll(turned[m], m + 4, 1), out)
    return out


def to_rows(v):
    even = jnp.stack([v[:, 256 * t : 256 * t + 128] for t in range(8)])
    odd = jnp.stack([v[:, 256 * t + 128 : 256 * t + 256] for t in range(8)])
    first = lax.broadcasted_iota(jnp.int32, even.shape, 1) < 4
    y0 = jnp.where(first, even, pltpu.roll(odd, 4, 1))
    y1 = jnp.where(first, pltpu.roll(even, 4, 1), odd)
    return jnp.concatenate(
        [block_transpose(y0).reshape(64, 128), block_transpose(y1).reshape(64, 128)], axis=1
    )


def from_rows(r):
    y0 = block_transpose(r[:, :128].reshape(8, 8, 128))
    y1 = block_transpose(r[:, 128:].reshape(8, 8, 128))
    first = lax.broadcasted_iota(jnp.int32, y0.shape, 1) < 4
    even = jnp.where(first, y0, pltpu.roll(y1, 4, 1))
    odd = jnp.where(first, pltpu.roll(y0, 4, 1), y1)
    return jnp.concatenate([part[t] for t in range(8) for part in (even, odd)], axis=1)


def width_index(shape):
    return lax.broadcasted_iota(jnp.int32, shape, 0) % LAYER


def from_left(x):
    return jnp.where(width_index(x.shape) == 0, 0.0, pltpu.roll(x, 1, 0))


def from_right(x):
    return jnp.where(width_index(x.shape) == LAYER - 1, 0.0, pltpu.roll(x, x.shape[0] - 1, 0))


def kernel(
    crops,
    partner,
    inverse,
    vol,
    cot,
    kern,
    gvol,
    kg,
    kf,
    fwd_w,
    bwd_w,
    ext,
    cotr,
    slope1,
    slope2,
    part,
    pieces_out,
    pieces_in,
    mixed_out,
    mixed_in,
    kg_send,
    kg_recv,
    kg_pair,
    kg_all,
    halo_send,
    halo_recv,
    a2a_send,
    a2a_recv,
    pair_sems,
    all_send,
    all_recv,
):
    me = lax.axis_index("sample")
    d = lax.axis_index("depth")
    core = lax.rem(d, 2)
    mate = d + 1 - 2 * core
    far = lax.rem(d + 2, 4)
    far_mate = lax.rem(mate + 2, 4)

    barrier = pltpu.get_barrier_semaphore()

    @pl.loop(1, crops)
    def _(k):
        peer = lax.rem(me + k, crops)
        pl.semaphore_signal(barrier, inc=1, device_id=(peer, d), device_id_type=MESH)

    for k in (1, 2, 3):
        pl.semaphore_signal(
            barrier, inc=1, device_id=(me, lax.rem(d + k, 4)), device_id_type=MESH
        )

    for layer in range(4):
        ext[0, LAYER * (layer + 1) : LAYER * (layer + 2), :] = to_rows(
            vol[0, layer].astype(F32)
        ).astype(BF16)

    @pl.when(d == 0)
    def _():
        for k in range(6):
            ext[k, 0:LAYER, :] = jnp.zeros((LAYER, LANES), BF16)

    @pl.when(d == 3)
    def _():
        for k in range(6):
            ext[k, 5 * LAYER : 6 * LAYER, :] = jnp.zeros((LAYER, LANES), BF16)

    for l in range(3):
        kf[l] = kern[l].astype(F32)

    sub = lax.broadcasted_iota(jnp.int32, (8, 128), 0)
    blk8 = lax.broadcasted_iota(jnp.int32, (8, 128), 1) // 32
    blk32 = lax.broadcasted_iota(jnp.int32, (32, 128), 1) // 32

    def build(l):
        @pl.loop(0, 9)
        def _(ac):
            a = ac // 3
            c = lax.rem(ac, 3)
            taps = []
            for b in range(3):
                row = kf[l, pl.ds(9 * a + 3 * b + c, 1), :]
                tiles = []
                for r in range(4):
                    low = jnp.broadcast_to(row[:, 256 * r : 256 * r + 128], (8, 128))
                    high = jnp.broadcast_to(row[:, 256 * r + 128 : 256 * r + 256], (8, 128))
                    z = jnp.where(blk8 == sub % 4, jnp.where(sub < 4, low, high), 0.0)
                    z = z + pltpu.roll(z, 64, 1)
                    tiles.append(z + pltpu.roll(z, 32, 1))
                taps.append(jnp.concatenate(tiles, axis=0))
            row0 = pl.multiple_of(a * 256, 256)
            for hp in range(8):
                for j in range(2):
                    block = jnp.zeros((32, 128), F32)
                    for b in range(3):
                        h = hp - b + 1
                        if h // 4 == j and 0 <= h < 8:
                            block = jnp.where(blk32 == h % 4, taps[b], block)
                    block = block.astype(BF16)
                    rows = pl.ds(pl.multiple_of(row0 + 32 * hp, 32), 32)
                    fwd_w[l, c, rows, 128 * j : 128 * j + 128] = block
                    bwd_w[l, c, 32 * hp : 32 * hp + 32, pl.ds(pl.multiple_of(row0 + 128 * j, 128), 128)] = block

    def conv(x, l, starts, forward):
        if forward:
            order = (0, 1, 2)
        else:
            order = (2, 1, 0)
        lhs = jnp.concatenate(
            [
                jnp.concatenate(
                    [ext[x, LAYER * (s + a) : LAYER * (s + a + 1), :] for s in starts], axis=0
                )
                for a in order
            ],
            axis=1,
        )
        if forward:
            outs = [jnp.dot(lhs, fwd_w[l, c], preferred_element_type=F32) for c in range(3)]
            return outs[1] + from_left(outs[0]) + from_right(outs[2])
        outs = [
            lax.dot_general(lhs, bwd_w[l, c], NT, preferred_element_type=F32) for c in range(3)
        ]
        return outs[1] + from_right(outs[0]) + from_left(outs[2])

    def halo_copies(x):
        low = pltpu.make_async_remote_copy(
            src_ref=ext.at[x, pl.ds(LAYER, LAYER), :],
            dst_ref=ext.at[x, pl.ds(5 * LAYER, LAYER), :],
            send_sem=halo_send.at[x, 0],
            recv_sem=halo_recv.at[x, 1],
            device_id=(me, lax.rem(d + 3, 4)),
            device_id_type=MESH,
        )
        high = pltpu.make_async_remote_copy(
            src_ref=ext.at[x, pl.ds(4 * LAYER, LAYER), :],
            dst_ref=ext.at[x, pl.ds(0, LAYER), :],
            send_sem=halo_send.at[x, 1],
            recv_sem=halo_recv.at[x, 0],
            device_id=(me, lax.rem(d + 1, 4)),
            device_id_type=MESH,
        )
        return low, high

    def halo_start(x):
        low, high = halo_copies(x)

        @pl.when(d > 0)
        def _():
            low.start()

        @pl.when(d < 3)
        def _():
            high.start()

    def halo_wait(x):
        low, high = halo_copies(x)

        @pl.when(d > 0)
        def _():
            low.wait_send()
            high.wait_recv()

        @pl.when(d < 3)
        def _():
            high.wait_send()
            low.wait_recv()

    def fill_pieces(slot, values, rows_from):
        n = values.shape[0] // 8
        at = rows_from // 8
        for j in range(2):
            pieces_out[slot, 32 * j + at : 32 * j + at + n] = (
                values[:, 128 * j : 128 * j + 128].reshape(n, 8, 128).astype(BF16)
            )

    def scatter_start(slot, phase, source, target):
        @pl.loop(1, crops)
        def _(k):
            peer = lax.rem(me + k, crops)
            pltpu.make_async_remote_copy(
                src_ref=source.at[slot, peer],
                dst_ref=target.at[slot, me],
                send_sem=a2a_send.at[slot, phase],
                recv_sem=a2a_recv.at[slot, phase],
                device_id=(peer, d),
                device_id_type=MESH,
            ).start()

        target[slot, me] = source[slot, me]

    def scatter_wait(slot, phase, source, target):
        copy = pltpu.make_async_remote_copy(
            src_ref=source.at[slot, pl.ds(0, crops - 1)],
            dst_ref=target.at[slot, pl.ds(0, crops - 1)],
            send_sem=a2a_send.at[slot, phase],
            recv_sem=a2a_recv.at[slot, phase],
            device_id=(me, mate),
            device_id_type=MESH,
        )
        copy.wait()

    def joined(slot):
        whole = mixed_in[slot].astype(F32)
        return jnp.concatenate(
            [whole[0:32].reshape(ROWS, 128), whole[32:64].reshape(ROWS, 128)], axis=1
        )

    def kernel_grad(l, x, g):
        stacked = jnp.concatenate(
            [from_right(g).astype(BF16), g.astype(BF16), from_left(g).astype(BF16)], axis=1
        )
        for a in range(3):
            u = ext[x, LAYER * a : LAYER * a + ROWS, :]
            for c in range(3):
                r = lax.dot_general(
                    u, stacked[:, 256 * c : 256 * c + 256], TN, preferred_element_type=F32
                )

                def at(hp, j):
                    return r[32 * hp : 32 * hp + 32, 128 * j : 128 * j + 128]

                g0 = at(1, 0) + at(5, 1)
                g1 = at(2, 0) + at(6, 1)
                g2 = jnp.where(blk32 >= 2, at(3, 0) + at(7, 1), at(3, 1))
                g3 = jnp.where(blk32 == 3, at(4, 0), at(4, 1) + jnp.where(blk32 < 2, at(0, 0), 0.0))
                total = (
                    g0 + pltpu.roll(g1, 96, 1) + pltpu.roll(g2, 64, 1) + pltpu.roll(g3, 32, 1)
                )
                part[l, 0, 3 * a + c] = total[0:16]
                part[l, 1, 3 * a + c] = total[16:32]
        kg_send[l] = part[l, 1 - core].astype(BF16)

    def pair_copy(l):
        return pltpu.make_async_remote_copy(
            src_ref=kg_send.at[l],
            dst_ref=kg_recv.at[l],
            send_sem=pair_sems.at[l, 0],
            recv_sem=pair_sems.at[l, 1],
            device_id=(me, mate),
            device_id_type=MESH,
        )

    def all_copies(l):
        return [
            pltpu.make_async_remote_copy(
                src_ref=kg_pair.at[l],
                dst_ref=kg_all.at[l, k],
                send_sem=all_send.at[l, k],
                recv_sem=all_recv.at[l, k],
                device_id=(me, to),
                device_id_type=MESH,
            )
            for k, to in enumerate((mate, far, far_mate))
        ]

    def reduce_pairs(l):
        pair_copy(l).wait()
        kg_pair[l] = (part[l, core] + kg_recv[l].astype(F32)).astype(BF16)
        for copy in all_copies(l):
            copy.start()

    def reduce_finish(l):
        for copy in all_copies(l):
            copy.wait()
        own = kg_pair[l].astype(F32) + kg_all[l, 1].astype(F32)
        other = kg_all[l, 0].astype(F32) + kg_all[l, 2].astype(F32)
        kg[l, core] = own
        kg[l, 1 - core] = other

    build(0)
    pl.semaphore_wait(barrier, crops - 1 + 3)

    halo_start(0)
    inner, outer = (1, 2), (0, 3)

    def store_inner(ref, values):
        ref[LAYER : 3 * LAYER, :] = values

    def store_outer(ref, values):
        ref[0:LAYER, :] = values[0:LAYER]
        ref[3 * LAYER :, :] = values[LAYER:]

    def first_layer(starts):
        v = conv(0, 0, starts, True)
        s = logistic(v)
        hidden = v * s
        slope = s * (1.0 + v * (1.0 - s))
        if starts == inner:
            store_inner(slope1, slope)
            fill_pieces(0, hidden, LAYER)
        else:
            store_outer(slope1, slope)
            fill_pieces(0, hidden[0:LAYER], 0)
            fill_pieces(0, hidden[LAYER:], 3 * LAYER)

    first_layer(inner)
    build(1)
    halo_wait(0)
    first_layer(outer)

    scatter_start(0, 0, pieces_out, pieces_in)
    build(2)
    for layer in range(4):
        cotr[LAYER * layer : LAYER * (layer + 1), :] = to_rows(cot[0, layer].astype(F32)).astype(
            BF16
        )
    scatter_wait(0, 0, pieces_out, pieces_in)

    def blend(n, carry):
        own = pieces_in[0, n].astype(F32)
        other = pieces_in[0, partner[n]].astype(F32)
        mixed_out[0, n] = (OWN_SHARE * own + PARTNER_SHARE * other).astype(BF16)
        return carry

    lax.fori_loop(0, crops, blend, 0, unroll=8)
    scatter_start(0, 1, mixed_out, mixed_in)
    scatter_wait(0, 1, mixed_out, mixed_in)
    ext[1, LAYER : 5 * LAYER, :] = joined(0).astype(BF16)
    halo_start(1)

    def second_layer(starts):
        v = conv(1, 1, starts, True)
        s = logistic(v)
        second = (v * s).astype(BF16)
        slope = s * (1.0 + v * (1.0 - s))
        at = ext.at[2, pl.ds(LAYER, ROWS), :]
        if starts == inner:
            store_inner(slope2, slope)
            store_inner(at, second)
        else:
            store_outer(slope2, slope)
            store_outer(at, second)

    second_layer(inner)
    halo_wait(1)
    second_layer(outer)
    halo_start(2)

    def third_layer(starts):
        v = conv(2, 2, starts, True)
        s = logistic(v)
        slope = s * (1.0 + v * (1.0 - s))
        at = ext.at[3, pl.ds(LAYER, ROWS), :]
        if starts == inner:
            store_inner(at, (cotr[LAYER : 3 * LAYER, :].astype(F32) * slope).astype(BF16))
        else:
            facing = jnp.concatenate([cotr[0:LAYER, :], cotr[3 * LAYER :, :]], axis=0)
            store_outer(at, (facing.astype(F32) * slope).astype(BF16))

    third_layer(inner)
    halo_wait(2)
    third_layer(outer)
    halo_start(3)

    def back_three(starts):
        g = conv(3, 2, starts, False)
        at = ext.at[4, pl.ds(LAYER, ROWS), :]
        if starts == inner:
            store_inner(at, (g * slope2[LAYER : 3 * LAYER, :]).astype(BF16))
        else:
            facing = jnp.concatenate([slope2[0:LAYER, :], slope2[3 * LAYER :, :]], axis=0)
            store_outer(at, (g * facing).astype(BF16))

    back_three(inner)
    kernel_grad(2, 2, ext[3, LAYER : 5 * LAYER, :].astype(F32))
    halo_wait(3)
    back_three(outer)
    halo_start(4)
    pair_copy(2).start()

    g = conv(4, 1, inner, False)
    fill_pieces(1, g, LAYER)
    halo_wait(4)
    g = conv(4, 1, outer, False)
    fill_pieces(1, g[0:LAYER], 0)
    fill_pieces(1, g[LAYER:], 3 * LAYER)
    scatter_start(1, 0, pieces_out, pieces_in)
    reduce_pairs(2)
    kernel_grad(1, 1, ext[4, LAYER : 5 * LAYER, :].astype(F32))
    pair_copy(1).start()
    scatter_wait(1, 0, pieces_out, pieces_in)

    def blend_back(n, carry):
        own = pieces_in[1, n].astype(F32)
        other = pieces_in[1, inverse[n]].astype(F32)
        mixed_out[1, n] = (OWN_SHARE * own + PARTNER_SHARE * other).astype(BF16)
        return carry

    lax.fori_loop(0, crops, blend_back, 0, unroll=8)
    scatter_start(1, 1, mixed_out, mixed_in)
    reduce_pairs(1)
    reduce_finish(2)
    scatter_wait(1, 1, mixed_out, mixed_in)

    g_one = joined(1) * slope1[...]
    ext[5, LAYER : 5 * LAYER, :] = g_one.astype(BF16)
    halo_start(5)
    kernel_grad(0, 0, ext[5, LAYER : 5 * LAYER, :].astype(F32))
    pair_copy(0).start()
    g = conv(5, 0, inner, False)
    gvol[0, 1] = from_rows(g[0:LAYER]).astype(BF16)
    gvol[0, 2] = from_rows(g[LAYER:]).astype(BF16)
    reduce_pairs(0)
    halo_wait(5)
    g = conv(5, 0, outer, False)
    gvol[0, 0] = from_rows(g[0:LAYER]).astype(BF16)
    gvol[0, 3] = from_rows(g[LAYER:]).astype(BF16)
    reduce_finish(1)
    reduce_finish(0)


def per_device(crops, volume, kernels, partner, cotangent):
    order = jnp.arange(crops, dtype=jnp.int32)
    inverse = jnp.sum(
        jnp.where(partner[None, :] == order[:, None], order[None, :], 0), axis=1, dtype=jnp.int32
    )
    vmem = pl.BlockSpec(memory_space=pltpu.VMEM)
    smem = pl.BlockSpec(memory_space=pltpu.SMEM)
    dma = pltpu.SemaphoreType.DMA
    grad_volume, kg = pl.pallas_call(
        functools.partial(kernel, crops),
        out_shape=(
            jax.ShapeDtypeStruct((1, 4, 8, 2048), BF16),
            jax.ShapeDtypeStruct((3, 2, 9, 16, 128), F32),
        ),
        in_specs=[smem, smem, vmem, vmem, vmem],
        out_specs=(vmem, vmem),
        scratch_shapes=[
            pltpu.VMEM((3, 27, 1024), F32),
            pltpu.VMEM((3, 3, 768, 256), BF16),
            pltpu.VMEM((3, 3, 256, 768), BF16),
            pltpu.VMEM((6, 384, 256), BF16),
            pltpu.VMEM((256, 256), BF16),
            pltpu.VMEM((256, 256), F32),
            pltpu.VMEM((256, 256), F32),
            pltpu.VMEM((3, 2, 9, 16, 128), F32),
            pltpu.VMEM((2, crops, 8, 128), BF16),
            pltpu.VMEM((2, crops, 8, 128), BF16),
            pltpu.VMEM((2, crops, 8, 128), BF16),
            pltpu.VMEM((2, crops, 8, 128), BF16),
            pltpu.VMEM((3, 9, 16, 128), BF16),
            pltpu.VMEM((3, 9, 16, 128), BF16),
            pltpu.VMEM((3, 9, 16, 128), BF16),
            pltpu.VMEM((3, 3, 9, 16, 128), BF16),
            dma((6, 2)),
            dma((6, 2)),
            dma((2, 2)),
            dma((2, 2)),
            dma((3, 2)),
            dma((3, 3)),
            dma((3, 3)),
        ],
        compiler_params=pltpu.CompilerParams(
            collective_id=0, has_side_effects=True, vmem_limit_bytes=48 * 1024 * 1024
        ),
    )(partner, inverse, volume, cotangent, kernels)
    kg = kg[..., :96].reshape(3, 2, 3, 3, 16, 3, CH)[:, :, :, :, :, ::-1]
    kg = jnp.transpose(kg, (0, 2, 5, 3, 1, 4, 6)).reshape(1, 3, 27, CH * CH)
    return grad_volume, kg


def solution(mesh):
    crops = mesh.shape["sample"]
    in_specs = (P("sample", "depth", None, None), P(), P(), P("sample", "depth", None, None))
    out_specs = (P("sample", "depth", None, None), P("sample", None, None, None))
    return jax.shard_map(
        functools.partial(per_device, crops),
        mesh=mesh,
        in_specs=in_specs,
        out_specs=out_specs,
        check_vma=False,
    )
```

profile of v0, /device:TPU:1, one launch (start us, length us, event | category | flops | bytes accessed | tf_op | source)
XLA Modules:
  0.0 88.0 jit_solution(10123128627676761466)
XLA Ops:
  0.6 0.8 select_reduce_fusion.inverse
  1.4 0.0 copy-start
  1.4 0.9 %copy-done = bf16[3,27,1024]{2,1,0:T(8,128)(2,1)S(1)} copy-done((bf16[3,27,1024]{2,1,0:T(8,128)(2,1)S(1)}, bf16[3,27,1024]{2,1,0:T(8,128)(2,1)}, u32[]{:S(2)}) %copy-start) | copy-done | bytes 165912
  2.3 0.0 copy-start.1
  2.3 0.9 %copy-done.1 = bf16[1,4,8,2048]{3,2,1,0:T(8,128)(2,1)S(1)} copy-done((bf16[1,4,8,2048]{3,2,1,0:T(8,128)(2,1)S(1)}, bf16[1,4,8,2048]{3,2,1,0:T(8,128)(2,1)}, u32[]{:S(2)}) %copy-start.1) | copy-done | bytes 131096
  3.2 0.0 copy-start.2
  3.2 0.9 %copy-done.2 = bf16[1,4,8,2048]{3,2,1,0:T(8,128)(2,1)S(1)} copy-done((bf16[1,4,8,2048]{3,2,1,0:T(8,128)(2,1)S(1)}, bf16[1,4,8,2048]{3,2,1,0:T(8,128)(2,1)}, u32[]{:S(2)}) %copy-start.2) | copy-done | bytes 131096
  4.1 0.0 copy-start.3
  4.1 0.7 copy-done.3
  4.8 74.2 %shard_map.59 = (bf16[1,4,8,2048]{3,2,1,0:T(8,128)(2,1)S(1)}, f32[3,2,9,16,128]{4,3,2,1,0:T(8,128)S(1)}) custom-call(s32[64]{0:T(128)S(1)} %copy-done.3, s32[64]{0:T(128)S(1)} %select_reduce_fusion.inverse, bf16[1,4,8,2048]{3,2,1,0:T(8,128)(2,1)S(1)} %copy-done.1, bf16[1,4,8,2048]{3,2,1,0:T(8,128)(2,1)S(1)} %copy-done.2, bf16[3,27,1024]{2,1,0:T(8,128)(2,1)S(1)} %copy-done), custom_call_target="tpu_custom_call" | custom-call | tf_op jit(solution)/shard_map/pallas_call | solution.py:491
  79.0 1.9 %reshape.11 = f32[3,2,3,3,16,3,32]{6,5,4,3,2,1,0:T(4,128)} reshape(f32[3,2,9,16,96]{4,3,2,1,0:T(8,128)S(1)} %bitcast.6) | data formatting | bytes 663552 | tf_op jit(solution)/shard_map/reshape | solution.py:528
  80.8 5.0 %rev.3 = f32[3,2,3,3,16,3,32]{6,5,4,3,2,1,0:T(4,128)S(1)} reverse(f32[3,2,3,3,16,3,32]{6,5,4,3,2,1,0:T(4,128)} %reshape.11), dimensions={5} | reverse | bytes 663552 | tf_op jit(solution)/shard_map/rev | solution.py:528
  85.8 0.2 copy.9
  86.0 1.3 %reshape.13 = f32[1,3,27,1024]{3,0,2,1:T(1,128)} reshape(f32[3,3,3,3,2,16,32]{6,5,4,3,2,1,0:T(8,128)S(1)} %copy.9) | data formatting | bytes 663552 | tf_op jit(solution)/shard_map/reshape | solution.py:529
  87.3 0.7 copy.12
Async XLA Ops:
  1.4 0.9 %copy-start = (bf16[3,27,1024]{2,1,0:T(8,128)(2,1)S(1)}, bf16[3,27,1024]{2,1,0:T(8,128)(2,1)}, u32[]{:S(2)}) copy-start(bf16[3,27,1024]{2,1,0:T(8,128)(2,1)} %kern.1) | copy-start | bytes 497668
  2.3 0.9 %copy-start.1 = (bf16[1,4,8,2048]{3,2,1,0:T(8,128)(2,1)S(1)}, bf16[1,4,8,2048]{3,2,1,0:T(8,128)(2,1)}, u32[]{:S(2)}) copy-start(bf16[1,4,8,2048]{3,2,1,0:T(8,128)(2,1)} %vol.1) | copy-start | bytes 393220
  3.2 0.9 %copy-start.2 = (bf16[1,4,8,2048]{3,2,1,0:T(8,128)(2,1)S(1)}, bf16[1,4,8,2048]{3,2,1,0:T(8,128)(2,1)}, u32[]{:S(2)}) copy-start(bf16[1,4,8,2048]{3,2,1,0:T(8,128)(2,1)} %cot.1) | copy-start | bytes 393220
  4.1 0.7 copy-start.3
where the time goes:
time: 88.2 us; the launch traced here: 88 us
  Pallas kernels  74.2 us (84%)
  local copies, waits for them, and re-layouts  12.4 us (14%)
    pallas_call x1, Pallas kernels, per_device(): pl.pallas_call(functools.partial(kernel, crops), out_shape=(jax.ShapeDtyp...  74.2 us
    rev x1, local copies, waits for them, and re-layouts, per_device(): kg = kg[..., :96].reshape(3, 2, 3, 3, 16, 3, CH)[:, :, :, :, :, ::-1]  4.98 us
    unnamed x9, local copies, waits for them, and re-layouts  4.05 us
    reshape x1, local copies, waits for them, and re-layouts, per_device(): kg = kg[..., :96].reshape(3, 2, 3, 3, 16, 3, CH)[:, :, :, :, :, ::-1]  1.86 us

commit v1 on v0

--- a/solution.py
+++ b/solution.py
@@ -70,13 +70,19 @@
 
 def kernel(
     crops,
+    partner_hbm,
+    vol_hbm,
+    cot_hbm,
+    kern_hbm,
+    gvol,
+    kg,
     partner,
+    partner_row,
+    inverse_rows,
     inverse,
     vol,
     cot,
     kern,
-    gvol,
-    kg,
     kf,
     fwd_w,
     bwd_w,
@@ -100,7 +106,23 @@
     pair_sems,
     all_send,
     all_recv,
+    load_sems,
 ):
+    loads = [
+        pltpu.make_async_copy(source, target, load_sems.at[k])
+        for k, (source, target) in enumerate(
+            (
+                (vol_hbm, vol),
+                (kern_hbm, kern),
+                (partner_hbm, partner_row),
+                (partner_hbm, partner),
+                (cot_hbm, cot),
+            )
+        )
+    ]
+    turn = pltpu.make_async_copy(inverse_rows, inverse, load_sems.at[5])
+    for load in loads:
+        load.start()
     me = lax.axis_index("sample")
     d = lax.axis_index("depth")
     core = lax.rem(d, 2)
@@ -120,6 +142,7 @@
             barrier, inc=1, device_id=(me, lax.rem(d + k, 4)), device_id_type=MESH
         )
 
+    loads[0].wait()
     for layer in range(4):
         ext[0, LAYER * (layer + 1) : LAYER * (layer + 2), :] = to_rows(
             vol[0, layer].astype(F32)
@@ -135,12 +158,16 @@
         for k in range(6):
             ext[k, 5 * LAYER : 6 * LAYER, :] = jnp.zeros((LAYER, LANES), BF16)
 
+    loads[1].wait()
     for l in range(3):
         kf[l] = kern[l].astype(F32)
 
     sub = lax.broadcasted_iota(jnp.int32, (8, 128), 0)
     blk8 = lax.broadcasted_iota(jnp.int32, (8, 128), 1) // 32
+    sub32 = lax.broadcasted_iota(jnp.int32, (32, 128), 0) % 4
     blk32 = lax.broadcasted_iota(jnp.int32, (32, 128), 1) // 32
+
+    diagonal = [(sub32 == q) & (blk32 == q) for q in range(4)]
 
     def build(l):
         @pl.loop(0, 9)
@@ -335,10 +362,40 @@
             copy.wait()
         own = kg_pair[l].astype(F32) + kg_all[l, 1].astype(F32)
         other = kg_all[l, 0].astype(F32) + kg_all[l, 2].astype(F32)
-        kg[l, core] = own
-        kg[l, 1 - core] = other
+        for a in range(3):
+            for c in range(3):
+                k = 3 * a + c
+                x = jnp.concatenate(
+                    [
+                        jnp.where(core == 0, own[k], other[k]),
+                        jnp.where(core == 0, other[k], own[k]),
+                    ],
+                    axis=0,
+                )
+                turned = [x] + [pltpu.roll(x, 32 * m, 1) for m in (1, 2, 3)]
+                for b in range(3):
+                    z = jnp.zeros_like(x)
+                    for q in range(4):
+                        z = jnp.where(diagonal[q], turned[(q - 2 + b) % 4], z)
+                    z = z.reshape(4, 8, 128)
+                    z = z + pltpu.roll(z, 7, 1)
+                    z = z + pltpu.roll(z, 6, 1)
+                    t = 27 * l + 9 * a + 3 * b + c
+                    for r in range(4):
+                        kg[t, 2 * r : 2 * r + 1, :] = z[r, 0:1, :]
+                        kg[t, 2 * r + 1 : 2 * r + 2, :] = z[r, 4:5, :]
 
     build(0)
+    for load in loads[2:]:
+        load.wait()
+    shape = (crops, crops)
+    named = partner_row[...] == lax.broadcasted_iota(jnp.int32, shape, 0)
+    found = jnp.where(named, lax.broadcasted_iota(jnp.int32, shape, 1), 0)
+    inverse_rows[...] = jnp.broadcast_to(
+        jnp.minimum(jnp.sum(found, axis=1, keepdims=True, dtype=jnp.int32), crops - 1),
+        (crops, 128),
+    )
+    turn.start()
     pl.semaphore_wait(barrier, crops - 1 + 3)
 
     halo_start(0)
@@ -379,7 +436,7 @@
 
     def blend(n, carry):
         own = pieces_in[0, n].astype(F32)
-        other = pieces_in[0, partner[n]].astype(F32)
+        other = pieces_in[0, partner[0, n]].astype(F32)
         mixed_out[0, n] = (OWN_SHARE * own + PARTNER_SHARE * other).astype(BF16)
         return carry
 
@@ -451,9 +508,11 @@
     pair_copy(1).start()
     scatter_wait(1, 0, pieces_out, pieces_in)
 
+    turn.wait()
+
     def blend_back(n, carry):
         own = pieces_in[1, n].astype(F32)
-        other = pieces_in[1, inverse[n]].astype(F32)
+        other = pieces_in[1, inverse[n, 0]].astype(F32)
         mixed_out[1, n] = (OWN_SHARE * own + PARTNER_SHARE * other).astype(BF16)
         return carry
 
@@ -481,22 +540,25 @@
 
 
 def per_device(crops, volume, kernels, partner, cotangent):
-    order = jnp.arange(crops, dtype=jnp.int32)
-    inverse = jnp.sum(
-        jnp.where(partner[None, :] == order[:, None], order[None, :], 0), axis=1, dtype=jnp.int32
-    )
     vmem = pl.BlockSpec(memory_space=pltpu.VMEM)
-    smem = pl.BlockSpec(memory_space=pltpu.SMEM)
+    hbm = pl.BlockSpec(memory_space=pltpu.HBM)
     dma = pltpu.SemaphoreType.DMA
     grad_volume, kg = pl.pallas_call(
         functools.partial(kernel, crops),
         out_shape=(
             jax.ShapeDtypeStruct((1, 4, 8, 2048), BF16),
-            jax.ShapeDtypeStruct((3, 2, 9, 16, 128), F32),
+            jax.ShapeDtypeStruct((81, 8, 128), F32),
         ),
-        in_specs=[smem, smem, vmem, vmem, vmem],
+        in_specs=[hbm] * 4,
         out_specs=(vmem, vmem),
         scratch_shapes=[
+            pltpu.SMEM((1, crops), jnp.int32),
+            pltpu.VMEM((1, crops), jnp.int32),
+            pltpu.VMEM((crops, 128), jnp.int32),
+            pltpu.SMEM((crops, 128), jnp.int32),
+            pltpu.VMEM((1, 4, 8, 2048), BF16),
+            pltpu.VMEM((1, 4, 8, 2048), BF16),
+            pltpu.VMEM((3, 27, 1024), BF16),
             pltpu.VMEM((3, 27, 1024), F32),
             pltpu.VMEM((3, 3, 768, 256), BF16),
             pltpu.VMEM((3, 3, 256, 768), BF16),
@@ -520,14 +582,13 @@
             dma((3, 2)),
             dma((3, 3)),
             dma((3, 3)),
+            dma((6,)),
         ],
         compiler_params=pltpu.CompilerParams(
             collective_id=0, has_side_effects=True, vmem_limit_bytes=48 * 1024 * 1024
         ),
-    )(partner, inverse, volume, cotangent, kernels)
-    kg = kg[..., :96].reshape(3, 2, 3, 3, 16, 3, CH)[:, :, :, :, :, ::-1]
-    kg = jnp.transpose(kg, (0, 2, 5, 3, 1, 4, 6)).reshape(1, 3, 27, CH * CH)
-    return grad_volume, kg
+    )(*(pltpu.with_memory_space_constraint(x, pltpu.HBM) for x in (partner[None, :], volume, cotangent, kernels)))
+    return grad_volume, kg.reshape(1, 3, 27, CH * CH)
 
 
 def solution(mesh):

time: 88.2 us -> 76.2 us (0.86)
  local copies, waits for them, and re-layouts: 12.4 us -> 1.38 us
    rev x1 -> x0, local copies, waits for them, and re-layouts: 4.98 us -> none  [per_device(): kg = kg[..., :96].reshape(3, 2, 3, 3, 16, 3, CH)[:, :, :, :, :, ::-1]]
    reshape x2 -> x0, local copies, waits for them, and re-layouts: 3.18 us -> none  [the longest x1 1.86 us: per_device(): kg = kg[..., :96].reshape(3, 2, 3, 3, 16, 3, CH)[:, :, :, :, :, ::-1]]
    unnamed x9 -> x2, local copies, waits for them, and re-layouts: 4.05 us -> 1.38 us
where the time goes in v1:
time: 76.2 us; the launch traced here: 76.1 us
  Pallas kernels  74.1 us (97%)
  local copies, waits for them, and re-layouts  1.38 us (2%)
    pallas_call x1, Pallas kernels, per_device(): pl.pallas_call(functools.partial(kernel, crops), out_shape=(jax.ShapeDtyp...  74.1 us

profile of v1, /device:TPU:1, one launch (start us, length us, event | category | flops | bytes accessed | tf_op | source)
XLA Modules:
  0.0 76.1 jit_solution(4248800642568382612)
XLA Ops:
  0.6 74.1 %shard_map.59 = (bf16[1,4,8,2048]{3,2,1,0:T(8,128)(2,1)S(1)}, f32[81,8,128]{2,1,0:T(8,128)S(1)}) custom-call(s32[1,64]{1,0:T(1,128)} %bitcast.3, bf16[1,4,8,2048]{3,2,1,0:T(8,128)(2,1)} %vol_hbm.1, bf16[1,4,8,2048]{3,2,1,0:T(8,128)(2,1)} %cot_hbm.1, bf16[3,27,1024]{2,1,0:T(8,128)(2,1)} %kern_hbm.1), custom_call_target="tpu_custom_call" | custom-call | tf_op jit(solution)/shard_map/pallas_call | solution.py:546
  74.8 0.7 copy.10
  75.4 0.7 copy.11

commit v2 on v1

--- a/solution.py
+++ b/solution.py
@@ -87,7 +87,7 @@
     fwd_w,
     bwd_w,
     ext,
-    cotr,
+    wide,
     slope1,
     slope2,
     part,
@@ -95,12 +95,18 @@
     pieces_in,
     mixed_out,
     mixed_in,
+    far_in,
+    near_in,
     kg_send,
     kg_recv,
     kg_pair,
     kg_all,
     halo_send,
     halo_recv,
+    cot_send,
+    cot_recv,
+    far_sems,
+    near_sems,
     a2a_send,
     a2a_recv,
     pair_sems,
@@ -142,6 +148,15 @@
             barrier, inc=1, device_id=(me, lax.rem(d + k, 4)), device_id_type=MESH
         )
 
+    middle = (d == 1) | (d == 2)
+
+    @pl.when(middle)
+    def _():
+        @pl.loop(1, crops)
+        def _(k):
+            peer = lax.rem(me + k, crops)
+            pl.semaphore_signal(barrier, inc=1, device_id=(peer, 3 - d), device_id_type=MESH)
+
     loads[0].wait()
     for layer in range(4):
         ext[0, LAYER * (layer + 1) : LAYER * (layer + 2), :] = to_rows(
@@ -150,13 +165,15 @@
 
     @pl.when(d == 0)
     def _():
-        for k in range(6):
+        for k in range(2):
             ext[k, 0:LAYER, :] = jnp.zeros((LAYER, LANES), BF16)
+        wide[0, 0 : 4 * LAYER, :] = jnp.zeros((4 * LAYER, LANES), BF16)
 
     @pl.when(d == 3)
     def _():
-        for k in range(6):
+        for k in range(2):
             ext[k, 5 * LAYER : 6 * LAYER, :] = jnp.zeros((LAYER, LANES), BF16)
+        wide[0, 8 * LAYER : 12 * LAYER, :] = jnp.zeros((4 * LAYER, LANES), BF16)
 
     loads[1].wait()
     for l in range(3):
@@ -167,58 +184,80 @@
     sub32 = lax.broadcasted_iota(jnp.int32, (32, 128), 0) % 4
     blk32 = lax.broadcasted_iota(jnp.int32, (32, 128), 1) // 32
 
+    first_rows = (
+        lax.broadcasted_iota(jnp.int32, (32, 128), 0) == lax.broadcasted_iota(jnp.int32, (32, 128), 1)
+    ).astype(F32).astype(BF16)
     diagonal = [(sub32 == q) & (blk32 == q) for q in range(4)]
 
-    def build(l):
-        @pl.loop(0, 9)
-        def _(ac):
-            a = ac // 3
-            c = lax.rem(ac, 3)
-            taps = []
-            for b in range(3):
-                row = kf[l, pl.ds(9 * a + 3 * b + c, 1), :]
-                tiles = []
-                for r in range(4):
-                    low = jnp.broadcast_to(row[:, 256 * r : 256 * r + 128], (8, 128))
-                    high = jnp.broadcast_to(row[:, 256 * r + 128 : 256 * r + 256], (8, 128))
-                    z = jnp.where(blk8 == sub % 4, jnp.where(sub < 4, low, high), 0.0)
-                    z = z + pltpu.roll(z, 64, 1)
-                    tiles.append(z + pltpu.roll(z, 32, 1))
-                taps.append(jnp.concatenate(tiles, axis=0))
-            row0 = pl.multiple_of(a * 256, 256)
-            for hp in range(8):
-                for j in range(2):
-                    block = jnp.zeros((32, 128), F32)
-                    for b in range(3):
-                        h = hp - b + 1
-                        if h // 4 == j and 0 <= h < 8:
-                            block = jnp.where(blk32 == h % 4, taps[b], block)
-                    block = block.astype(BF16)
-                    rows = pl.ds(pl.multiple_of(row0 + 32 * hp, 32), 32)
-                    fwd_w[l, c, rows, 128 * j : 128 * j + 128] = block
-                    bwd_w[l, c, 32 * hp : 32 * hp + 32, pl.ds(pl.multiple_of(row0 + 128 * j, 128), 128)] = block
-
-    def conv(x, l, starts, forward):
+    def tap_tiles(l, a, c):
+        taps = []
+        for b in range(3):
+            row = kf[l, pl.ds(9 * a + 3 * b + c, 1), :]
+            tiles = []
+            for r in range(4):
+                low = jnp.broadcast_to(row[:, 256 * r : 256 * r + 128], (8, 128))
+                high = jnp.broadcast_to(row[:, 256 * r + 128 : 256 * r + 256], (8, 128))
+                z = jnp.where(blk8 == sub % 4, jnp.where(sub < 4, low, high), 0.0)
+                z = z + pltpu.roll(z, 64, 1)
+                tiles.append(z + pltpu.roll(z, 32, 1))
+            taps.append(jnp.concatenate(tiles, axis=0))
+        return taps
+
+    def store_blocks(target, l, a, c, taps, step):
+        row0 = pl.multiple_of(a * 256, 256)
+        for hp in range(8):
+            for j in range(2):
+                block = jnp.zeros((32, 128), F32)
+                for b in range(3):
+                    h = hp + step * (b - 1)
+                    if h // 4 == j and 0 <= h < 8:
+                        block = jnp.where(blk32 == h % 4, taps[b], block)
+                rows = pl.ds(pl.multiple_of(row0 + 32 * hp, 32), 32)
+                target[l, c, rows, 128 * j : 128 * j + 128] = block.astype(BF16)
+
+    def build(l, forward, backward):
+        @pl.loop(0, 3)
+        def _(a):
+            for c in range(3):
+                taps = tap_tiles(l, a, c)
+                if forward:
+                    store_blocks(fwd_w, l, a, c, taps, -1)
+                if backward:
+                    stacked = jnp.concatenate([tap for tap in taps for _ in range(4)], axis=0)
+                    back = lax.dot_general(
+                        first_rows, stacked.astype(BF16), NT, preferred_element_type=F32
+                    )
+                    store_blocks(
+                        bwd_w, l, a, c, [back[:, 128 * b : 128 * b + 128] for b in range(3)], 1
+                    )
+
+    def conv(x, l, ranges, forward):
+        lhs = []
+        for a in range(3):
+            shift = a - 1 if forward else 1 - a
+            lhs.append(
+                jnp.concatenate(
+                    [x[LAYER * (s + shift) : LAYER * (t + shift), :] for s, t in ranges], axis=0
+                )
+            )
+        lhs = jnp.concatenate(lhs, axis=1)
+        weights = fwd_w if forward else bwd_w
+        outs = [jnp.dot(lhs, weights[l, c], preferred_element_type=F32) for c in range(3)]
         if forward:
-            order = (0, 1, 2)
-        else:
-            order = (2, 1, 0)
-        lhs = jnp.concatenate(
-            [
-                jnp.concatenate(
-                    [ext[x, LAYER * (s + a) : LAYER * (s + a + 1), :] for s in starts], axis=0
-                )
-                for a in order
-            ],
-            axis=1,
-        )
-        if forward:
-            outs = [jnp.dot(lhs, fwd_w[l, c], preferred_element_type=F32) for c in range(3)]
             return outs[1] + from_left(outs[0]) + from_right(outs[2])
-        outs = [
-            lax.dot_general(lhs, bwd_w[l, c], NT, preferred_element_type=F32) for c in range(3)
-        ]
         return outs[1] + from_right(outs[0]) + from_left(outs[2])
+
+    def masked(values, s):
+        parts = []
+        n = values.shape[0] // LAYER
+        for k in range(n):
+            piece = values[LAYER * k : LAYER * (k + 1)]
+            if s + k < 4:
+                piece = jnp.where(d > 0, piece, 0.0)
+            elif s + k >= 8:
+                piece = jnp.where(d < 3, piece, 0.0)
+            parts.append(piece)
+        return jnp.concatenate(parts, axis=0)
 
     def halo_copies(x):
         low = pltpu.make_async_remote_copy(
@@ -271,10 +310,45 @@
                 values[:, 128 * j : 128 * j + 128].reshape(n, 8, 128).astype(BF16)
             )
 
+    def cot_copies():
+        low = pltpu.make_async_remote_copy(
+            src_ref=wide.at[4, pl.ds(4 * LAYER, 2 * LAYER), :],
+            dst_ref=wide.at[4, pl.ds(8 * LAYER, 2 * LAYER), :],
+            send_sem=cot_send.at[0],
+            recv_sem=cot_recv.at[1],
+            device_id=(me, lax.rem(d + 3, 4)),
+            device_id_type=MESH,
+        )
+        high = pltpu.make_async_remote_copy(
+            src_ref=wide.at[4, pl.ds(6 * LAYER, 2 * LAYER), :],
+            dst_ref=wide.at[4, pl.ds(2 * LAYER, 2 * LAYER), :],
+            send_sem=cot_send.at[1],
+            recv_sem=cot_recv.at[0],
+            device_id=(me, lax.rem(d + 1, 4)),
+            device_id_type=MESH,
+        )
+        return low, high
+
+    z = me // 16
+    spread = ((3 - z), lax.rem(z + 2, 4), z + 1 - 2 * lax.rem(z, 2), z)
+
+    ys = [lax.rem(me + 2 + k, 4) for k in range(4)]
+
+    def peers_of(zt, send, skip_own):
+        @pl.loop(0, 4)
+        def _(k):
+            row = 16 * zt + 4 * lax.rem(me // 4 + 2 + k, 4)
+            for at, y in enumerate(ys):
+                if skip_own and at == 2:
+
+                    @pl.when(k != 2)
+                    def _():
+                        send(row + y)
+                else:
+                    send(row + y)
+
     def scatter_start(slot, phase, source, target):
-        @pl.loop(1, crops)
-        def _(k):
-            peer = lax.rem(me + k, crops)
+        def send(peer):
             pltpu.make_async_remote_copy(
                 src_ref=source.at[slot, peer],
                 dst_ref=target.at[slot, me],
@@ -284,7 +358,47 @@
                 device_id_type=MESH,
             ).start()
 
+        for zt in spread:
+            peers_of(zt, send, zt is z)
         target[slot, me] = source[slot, me]
+
+    def far_start():
+        @pl.when(middle)
+        def _():
+            def send(peer):
+                pltpu.make_async_remote_copy(
+                    src_ref=mixed_out.at[0, peer],
+                    dst_ref=far_in.at[me],
+                    send_sem=far_sems.at[0],
+                    recv_sem=far_sems.at[1],
+                    device_id=(peer, 3 - d),
+                    device_id_type=MESH,
+                ).start()
+
+            for zt in spread[::-1]:
+                peers_of(zt, send, False)
+
+    def far_wait():
+        @pl.when(middle)
+        def _():
+            pltpu.make_async_remote_copy(
+                src_ref=mixed_out.at[0],
+                dst_ref=far_in,
+                send_sem=far_sems.at[0],
+                recv_sem=far_sems.at[1],
+                device_id=(me, mate),
+                device_id_type=MESH,
+            ).wait()
+
+    def near_copy():
+        return pltpu.make_async_remote_copy(
+            src_ref=mixed_in.at[0],
+            dst_ref=near_in,
+            send_sem=near_sems.at[0],
+            recv_sem=near_sems.at[1],
+            device_id=(me, mate),
+            device_id_type=MESH,
+        )
 
     def scatter_wait(slot, phase, source, target):
         copy = pltpu.make_async_remote_copy(
@@ -297,18 +411,18 @@
         )
         copy.wait()
 
-    def joined(slot):
-        whole = mixed_in[slot].astype(F32)
+    def joined(pieces):
+        whole = pieces.astype(F32)
         return jnp.concatenate(
             [whole[0:32].reshape(ROWS, 128), whole[32:64].reshape(ROWS, 128)], axis=1
         )
 
-    def kernel_grad(l, x, g):
+    def kernel_grad(l, x, first, g):
         stacked = jnp.concatenate(
             [from_right(g).astype(BF16), g.astype(BF16), from_left(g).astype(BF16)], axis=1
         )
         for a in range(3):
-            u = ext[x, LAYER * a : LAYER * a + ROWS, :]
+            u = x[LAYER * (first + a) : LAYER * (first + a) + ROWS, :]
             for c in range(3):
                 r = lax.dot_general(
                     u, stacked[:, 256 * c : 256 * c + 256], TN, preferred_element_type=F32
@@ -385,8 +499,8 @@
                         kg[t, 2 * r : 2 * r + 1, :] = z[r, 0:1, :]
                         kg[t, 2 * r + 1 : 2 * r + 2, :] = z[r, 4:5, :]
 
-    build(0)
-    for load in loads[2:]:
+    build(0, True, False)
+    for load in loads[2:4]:
         load.wait()
     shape = (crops, crops)
     named = partner_row[...] == lax.broadcasted_iota(jnp.int32, shape, 0)
@@ -396,42 +510,47 @@
         (crops, 128),
     )
     turn.start()
-    pl.semaphore_wait(barrier, crops - 1 + 3)
+    pl.semaphore_wait(barrier, crops + 2 + (crops - 1) * lax.rem((d + 1) // 2, 2))
+
+    xv, g1 = ext.at[0], ext.at[1]
+    xb, xs, g3, g2, cotr = (wide.at[k] for k in range(5))
 
     halo_start(0)
-    inner, outer = (1, 2), (0, 3)
-
-    def store_inner(ref, values):
-        ref[LAYER : 3 * LAYER, :] = values
-
-    def store_outer(ref, values):
-        ref[0:LAYER, :] = values[0:LAYER]
-        ref[3 * LAYER :, :] = values[LAYER:]
-
-    def first_layer(starts):
-        v = conv(0, 0, starts, True)
+
+    def first_layer(ranges):
+        v = conv(xv, 0, ranges, True)
         s = logistic(v)
         hidden = v * s
         slope = s * (1.0 + v * (1.0 - s))
-        if starts == inner:
-            store_inner(slope1, slope)
-            fill_pieces(0, hidden, LAYER)
-        else:
-            store_outer(slope1, slope)
-            fill_pieces(0, hidden[0:LAYER], 0)
-            fill_pieces(0, hidden[LAYER:], 3 * LAYER)
-
-    first_layer(inner)
-    build(1)
+        at = 0
+        for first, last in ranges:
+            n = LAYER * (last - first)
+            slope1[LAYER * (first - 1) : LAYER * (last - 1), :] = slope[at : at + n]
+            fill_pieces(0, hidden[at : at + n], LAYER * (first - 1))
+            at += n
+
+    first_layer(((2, 4),))
+    loads[4].wait()
+    for layer in range(4):
+        cotr[LAYER * (layer + 4) : LAYER * (layer + 5), :] = to_rows(
+            cot[0, layer].astype(F32)
+        ).astype(BF16)
+    build(1, True, False)
     halo_wait(0)
-    first_layer(outer)
+    first_layer(((1, 2), (4, 5)))
 
     scatter_start(0, 0, pieces_out, pieces_in)
-    build(2)
-    for layer in range(4):
-        cotr[LAYER * layer : LAYER * (layer + 1), :] = to_rows(cot[0, layer].astype(F32)).astype(
-            BF16
-        )
+    cot_low, cot_high = cot_copies()
+
+    @pl.when(d > 0)
+    def _():
+        cot_low.start()
+
+    @pl.when(d < 3)
+    def _():
+        cot_high.start()
+
+    build(2, True, True)
     scatter_wait(0, 0, pieces_out, pieces_in)
 
     def blend(n, carry):
@@ -441,73 +560,66 @@
         return carry
 
     lax.fori_loop(0, crops, blend, 0, unroll=8)
+    far_start()
     scatter_start(0, 1, mixed_out, mixed_in)
+    build(1, False, True)
+    build(0, False, True)
     scatter_wait(0, 1, mixed_out, mixed_in)
-    ext[1, LAYER : 5 * LAYER, :] = joined(0).astype(BF16)
-    halo_start(1)
-
-    def second_layer(starts):
-        v = conv(1, 1, starts, True)
-        s = logistic(v)
-        second = (v * s).astype(BF16)
-        slope = s * (1.0 + v * (1.0 - s))
-        at = ext.at[2, pl.ds(LAYER, ROWS), :]
-        if starts == inner:
-            store_inner(slope2, slope)
-            store_inner(at, second)
-        else:
-            store_outer(slope2, slope)
-            store_outer(at, second)
-
-    second_layer(inner)
-    halo_wait(1)
-    second_layer(outer)
-    halo_start(2)
-
-    def third_layer(starts):
-        v = conv(2, 2, starts, True)
-        s = logistic(v)
-        slope = s * (1.0 + v * (1.0 - s))
-        at = ext.at[3, pl.ds(LAYER, ROWS), :]
-        if starts == inner:
-            store_inner(at, (cotr[LAYER : 3 * LAYER, :].astype(F32) * slope).astype(BF16))
-        else:
-            facing = jnp.concatenate([cotr[0:LAYER, :], cotr[3 * LAYER :, :]], axis=0)
-            store_outer(at, (facing.astype(F32) * slope).astype(BF16))
-
-    third_layer(inner)
-    halo_wait(2)
-    third_layer(outer)
-    halo_start(3)
-
-    def back_three(starts):
-        g = conv(3, 2, starts, False)
-        at = ext.at[4, pl.ds(LAYER, ROWS), :]
-        if starts == inner:
-            store_inner(at, (g * slope2[LAYER : 3 * LAYER, :]).astype(BF16))
-        else:
-            facing = jnp.concatenate([slope2[0:LAYER, :], slope2[3 * LAYER :, :]], axis=0)
-            store_outer(at, (g * facing).astype(BF16))
-
-    back_three(inner)
-    kernel_grad(2, 2, ext[3, LAYER : 5 * LAYER, :].astype(F32))
-    halo_wait(3)
-    back_three(outer)
-    halo_start(4)
+    near_copy().start()
+    xb[4 * LAYER : 8 * LAYER, :] = joined(mixed_in[0]).astype(BF16)
+
+    def second_layer(s, t):
+        v = conv(xb, 1, ((s, t),), True)
+        gate = logistic(v)
+        xs[LAYER * s : LAYER * t, :] = masked(v * gate, s).astype(BF16)
+        slope2[LAYER * s : LAYER * t, :] = gate * (1.0 + v * (1.0 - gate))
+
+    second_layer(5, 7)
+    far_wait()
+
+    @pl.when(middle)
+    def _():
+        xb[pl.ds(pl.multiple_of(512 * core, 512), 256), :] = joined(far_in[...]).astype(BF16)
+
+    near_copy().wait()
+    xb[pl.ds(pl.multiple_of(512 * (1 - core), 512), 256), :] = joined(near_in[...]).astype(BF16)
+    second_layer(1, 5)
+    second_layer(7, 11)
+
+    @pl.when(d > 0)
+    def _():
+        cot_low.wait_send()
+        cot_high.wait_recv()
+
+    @pl.when(d < 3)
+    def _():
+        cot_high.wait_send()
+        cot_low.wait_recv()
+
+    def third_layer(s, t):
+        v = conv(xs, 2, ((s, t),), True)
+        gate = logistic(v)
+        slope = gate * (1.0 + v * (1.0 - gate))
+        facing = cotr[LAYER * s : LAYER * t, :].astype(F32)
+        g3[LAYER * s : LAYER * t, :] = masked(facing * slope, s).astype(BF16)
+
+    third_layer(2, 6)
+    third_layer(6, 10)
+
+    def back_three(s, t):
+        g = conv(g3, 2, ((s, t),), False) * slope2[LAYER * s : LAYER * t, :]
+        g2[LAYER * s : LAYER * t, :] = masked(g, s).astype(BF16)
+
+    back_three(3, 6)
+    back_three(6, 9)
+    fill_pieces(1, conv(g2, 1, ((4, 8),), False), 0)
+    scatter_start(1, 0, pieces_out, pieces_in)
+    kernel_grad(2, xs, 3, g3[4 * LAYER : 8 * LAYER, :].astype(F32))
     pair_copy(2).start()
-
-    g = conv(4, 1, inner, False)
-    fill_pieces(1, g, LAYER)
-    halo_wait(4)
-    g = conv(4, 1, outer, False)
-    fill_pieces(1, g[0:LAYER], 0)
-    fill_pieces(1, g[LAYER:], 3 * LAYER)
-    scatter_start(1, 0, pieces_out, pieces_in)
+    kernel_grad(1, xb, 3, g2[4 * LAYER : 8 * LAYER, :].astype(F32))
+    pair_copy(1).start()
     reduce_pairs(2)
-    kernel_grad(1, 1, ext[4, LAYER : 5 * LAYER, :].astype(F32))
-    pair_copy(1).start()
     scatter_wait(1, 0, pieces_out, pieces_in)
-
     turn.wait()
 
     def blend_back(n, carry):
@@ -522,17 +634,17 @@
     reduce_finish(2)
     scatter_wait(1, 1, mixed_out, mixed_in)
 
-    g_one = joined(1) * slope1[...]
-    ext[5, LAYER : 5 * LAYER, :] = g_one.astype(BF16)
-    halo_start(5)
-    kernel_grad(0, 0, ext[5, LAYER : 5 * LAYER, :].astype(F32))
+    g_one = (joined(mixed_in[1]) * slope1[...]).astype(BF16)
+    g1[LAYER : 5 * LAYER, :] = g_one
+    halo_start(1)
+    kernel_grad(0, xv, 0, g_one.astype(F32))
     pair_copy(0).start()
-    g = conv(5, 0, inner, False)
+    g = conv(g1, 0, ((2, 4),), False)
     gvol[0, 1] = from_rows(g[0:LAYER]).astype(BF16)
     gvol[0, 2] = from_rows(g[LAYER:]).astype(BF16)
     reduce_pairs(0)
-    halo_wait(5)
-    g = conv(5, 0, outer, False)
+    halo_wait(1)
+    g = conv(g1, 0, ((1, 2), (4, 5)), False)
     gvol[0, 0] = from_rows(g[0:LAYER]).astype(BF16)
     gvol[0, 3] = from_rows(g[LAYER:]).astype(BF16)
     reduce_finish(1)
@@ -561,22 +673,28 @@
             pltpu.VMEM((3, 27, 1024), BF16),
             pltpu.VMEM((3, 27, 1024), F32),
             pltpu.VMEM((3, 3, 768, 256), BF16),
-            pltpu.VMEM((3, 3, 256, 768), BF16),
-            pltpu.VMEM((6, 384, 256), BF16),
-            pltpu.VMEM((256, 256), BF16),
+            pltpu.VMEM((3, 3, 768, 256), BF16),
+            pltpu.VMEM((2, 384, 256), BF16),
+            pltpu.VMEM((5, 768, 256), BF16),
             pltpu.VMEM((256, 256), F32),
-            pltpu.VMEM((256, 256), F32),
+            pltpu.VMEM((768, 256), F32),
             pltpu.VMEM((3, 2, 9, 16, 128), F32),
             pltpu.VMEM((2, crops, 8, 128), BF16),
             pltpu.VMEM((2, crops, 8, 128), BF16),
             pltpu.VMEM((2, crops, 8, 128), BF16),
             pltpu.VMEM((2, crops, 8, 128), BF16),
+            pltpu.VMEM((crops, 8, 128), BF16),
+            pltpu.VMEM((crops, 8, 128), BF16),
             pltpu.VMEM((3, 9, 16, 128), BF16),
             pltpu.VMEM((3, 9, 16, 128), BF16),
             pltpu.VMEM((3, 9, 16, 128), BF16),
             pltpu.VMEM((3, 3, 9, 16, 128), BF16),
-            dma((6, 2)),
-            dma((6, 2)),
+            dma((2, 2)),
+            dma((2, 2)),
+            dma((2,)),
+            dma((2,)),
+            dma((2,)),
+            dma((2,)),
             dma((2, 2)),
             dma((2, 2)),
             dma((3, 2)),

time: 76.2 us -> 64.6 us (0.85)
  Pallas kernels: 74.1 us -> 62.5 us
    pallas_call x1, Pallas kernels: 74.1 us -> 62.5 us  [per_device(): pl.pallas_call(functools.partial(kernel, crops), out_shape=(jax.ShapeDtyp...]
where the time goes in v2:
time: 64.6 us; the launch traced here: 64.5 us
  Pallas kernels  62.5 us (97%)
  local copies, waits for them, and re-layouts  1.38 us (2%)
    pallas_call x1, Pallas kernels, per_device(): pl.pallas_call(functools.partial(kernel, crops), out_shape=(jax.ShapeDtyp...  62.5 us
    unnamed x2, local copies, waits for them, and re-layouts  1.38 us

profile of v2, /device:TPU:1, one launch (start us, length us, event | category | flops | bytes accessed | tf_op | source)
XLA Modules:
  0.0 64.5 jit_solution(10247099883080629627)
XLA Ops:
  0.6 62.5 %shard_map.59 = (bf16[1,4,8,2048]{3,2,1,0:T(8,128)(2,1)S(1)}, f32[81,8,128]{2,1,0:T(8,128)S(1)}) custom-call(s32[1,64]{1,0:T(1,128)} %bitcast.3, bf16[1,4,8,2048]{3,2,1,0:T(8,128)(2,1)} %vol_hbm.1, bf16[1,4,8,2048]{3,2,1,0:T(8,128)(2,1)} %cot_hbm.1, bf16[3,27,1024]{2,1,0:T(8,128)(2,1)} %kern_hbm.1), custom_call_target="tpu_custom_call" | custom-call | tf_op jit(solution)/shard_map/pallas_call | solution.py:658
  63.1 0.7 %copy.10 = bf16[1,4,8,2048]{3,2,1,0:T(8,128)(2,1)} copy(bf16[1,4,8,2048]{3,2,1,0:T(8,128)(2,1)S(1)} %get-tuple-element.12) | data formatting | bytes 262144
  63.8 0.7 %copy.11 = f32[1,3,27,1024]{3,0,2,1:T(1,128)} copy(f32[1,3,27,1024]{3,0,2,1:T(1,128)S(1)} %bitcast.2) | data formatting | bytes 663552

commit v3 on v2

--- a/solution.py
+++ b/solution.py
@@ -101,6 +101,8 @@
     kg_recv,
     kg_pair,
     kg_all,
+    kg_sum,
+    kg_shared,
     halo_send,
     halo_recv,
     cot_send,
@@ -112,6 +114,7 @@
     pair_sems,
     all_send,
     all_recv,
+    share_sems,
     load_sems,
 ):
     loads = [
@@ -136,26 +139,59 @@
     far = lax.rem(d + 2, 4)
     far_mate = lax.rem(mate + 2, 4)
 
+    z = me // 16
+    mid = (z == 1) | (z == 2)
+    middle = (d == 1) | (d == 2)
+    mid_count = lax.rem((z + 1) // 2, 2)
+    middle_count = lax.rem((d + 1) // 2, 2)
+    slot_here = me - 16
+    ys = [lax.rem(me + 2 + k, 4) for k in range(4)]
+    xs_far = me // 4 + 2
+
+    def peers_of(zt, send, skip_own):
+        @pl.loop(0, 4)
+        def _(k):
+            row = 16 * zt + 4 * lax.rem(xs_far + k, 4)
+            for at, y in enumerate(ys):
+                if skip_own and at == 2:
+
+                    @pl.when((k != 2) | (zt != z))
+                    def _():
+                        send(row + y)
+                else:
+                    send(row + y)
+
+    mids_first = 1 + mid_count * (2 - z) + (1 - mid_count) * (1 - z // 3)
+    mid_order = (mids_first, 3 - mids_first)
+    edge = 3 * (2 - z)
+    all_order = (edge, 3 - edge, 3 - z, z)
+    far_order = (z, 3 - z, 3 - edge, edge)
+
     barrier = pltpu.get_barrier_semaphore()
 
-    @pl.loop(1, crops)
-    def _(k):
-        peer = lax.rem(me + k, crops)
-        pl.semaphore_signal(barrier, inc=1, device_id=(peer, d), device_id_type=MESH)
+    def greet(depth):
+        def signal(peer):
+            pl.semaphore_signal(barrier, inc=1, device_id=(peer, depth), device_id_type=MESH)
+
+        return signal
+
+    for zt in mid_order:
+        peers_of(zt, greet(d), True)
+
+    @pl.when(mid)
+    def _():
+        for zt in (0, 3):
+            peers_of(zt, greet(d), False)
 
     for k in (1, 2, 3):
         pl.semaphore_signal(
             barrier, inc=1, device_id=(me, lax.rem(d + k, 4)), device_id_type=MESH
         )
 
-    middle = (d == 1) | (d == 2)
-
     @pl.when(middle)
     def _():
-        @pl.loop(1, crops)
-        def _(k):
-            peer = lax.rem(me + k, crops)
-            pl.semaphore_signal(barrier, inc=1, device_id=(peer, 3 - d), device_id_type=MESH)
+        for zt in mid_order:
+            peers_of(zt, greet(3 - d), True)
 
     loads[0].wait()
     for layer in range(4):
@@ -231,21 +267,33 @@
                         bwd_w, l, a, c, [back[:, 128 * b : 128 * b + 128] for b in range(3)], 1
                     )
 
-    def conv(x, l, ranges, forward):
-        lhs = []
-        for a in range(3):
-            shift = a - 1 if forward else 1 - a
-            lhs.append(
-                jnp.concatenate(
-                    [x[LAYER * (s + shift) : LAYER * (t + shift), :] for s, t in ranges], axis=0
-                )
-            )
-        lhs = jnp.concatenate(lhs, axis=1)
+    def at_rows(s, n):
+        start = LAYER * s
+        if not isinstance(s, int):
+            start = pl.multiple_of(start, LAYER)
+        return pl.ds(start, LAYER * n)
+
+    def taps_of(lhs, l, forward):
         weights = fwd_w if forward else bwd_w
         outs = [jnp.dot(lhs, weights[l, c], preferred_element_type=F32) for c in range(3)]
         if forward:
             return outs[1] + from_left(outs[0]) + from_right(outs[2])
         return outs[1] + from_right(outs[0]) + from_left(outs[2])
+
+    def conv(x, l, s, n, forward):
+        shifts = (-1, 0, 1) if forward else (1, 0, -1)
+        lhs = jnp.concatenate([x[at_rows(s + shift, n), :] for shift in shifts], axis=1)
+        return taps_of(lhs, l, forward)
+
+    def conv_ranges(x, l, ranges, forward):
+        shifts = (-1, 0, 1) if forward else (1, 0, -1)
+        lhs = [
+            jnp.concatenate(
+                [x[LAYER * (s + shift) : LAYER * (t + shift), :] for s, t in ranges], axis=0
+            )
+            for shift in shifts
+        ]
+        return taps_of(jnp.concatenate(lhs, axis=1), l, forward)
 
     def masked(values, s):
         parts = []
@@ -303,11 +351,11 @@
             low.wait_recv()
 
     def fill_pieces(slot, values, rows_from):
-        n = values.shape[0] // 8
-        at = rows_from // 8
+        n = values.shape[0] // 16
+        at = rows_from // 16
         for j in range(2):
-            pieces_out[slot, 32 * j + at : 32 * j + at + n] = (
-                values[:, 128 * j : 128 * j + 128].reshape(n, 8, 128).astype(BF16)
+            pieces_out[slot, 16 * j + at : 16 * j + at + n] = (
+                values[:, 128 * j : 128 * j + 128].astype(BF16).reshape(n, 16, 128)
             )
 
     def cot_copies():
@@ -329,66 +377,100 @@
         )
         return low, high
 
-    z = me // 16
-    spread = ((3 - z), lax.rem(z + 2, 4), z + 1 - 2 * lax.rem(z, 2), z)
-
-    ys = [lax.rem(me + 2 + k, 4) for k in range(4)]
-
-    def peers_of(zt, send, skip_own):
-        @pl.loop(0, 4)
-        def _(k):
-            row = 16 * zt + 4 * lax.rem(me // 4 + 2 + k, 4)
-            for at, y in enumerate(ys):
-                if skip_own and at == 2:
-
-                    @pl.when(k != 2)
-                    def _():
-                        send(row + y)
-                else:
-                    send(row + y)
-
-    def scatter_start(slot, phase, source, target):
+    def first_copy(slot, source, target, to):
+        return pltpu.make_async_remote_copy(
+            src_ref=source,
+            dst_ref=target,
+            send_sem=a2a_send.at[slot, 0],
+            recv_sem=a2a_recv.at[slot, 0],
+            device_id=(to, d),
+            device_id_type=MESH,
+        )
+
+    def scatter_start(slot):
         def send(peer):
-            pltpu.make_async_remote_copy(
-                src_ref=source.at[slot, peer],
-                dst_ref=target.at[slot, me],
-                send_sem=a2a_send.at[slot, phase],
-                recv_sem=a2a_recv.at[slot, phase],
-                device_id=(peer, d),
-                device_id_type=MESH,
+            first_copy(slot, pieces_out.at[slot, peer - 16], pieces_in.at[slot, me], peer).start()
+
+        for zt in mid_order:
+            peers_of(zt, send, True)
+
+        @pl.when(mid)
+        def _():
+            pieces_in[slot, me] = pieces_out[slot, slot_here]
+
+    def scatter_wait(slot):
+        @pl.when(mid)
+        def _():
+            span = pieces_in.at[slot, pl.ds(0, 31)]
+            first_copy(slot, pieces_out.at[slot, pl.ds(0, 31)], span, me).wait_send()
+            span = pieces_in.at[slot, pl.ds(0, crops - 1)]
+            first_copy(slot, span, span, me).wait_recv()
+
+        @pl.when(jnp.logical_not(mid))
+        def _():
+            span = pieces_in.at[slot, pl.ds(0, 32)]
+            first_copy(slot, pieces_out.at[slot], span, me).wait_send()
+
+    def second_copy(slot, source, target, to):
+        return pltpu.make_async_remote_copy(
+            src_ref=source,
+            dst_ref=target,
+            send_sem=a2a_send.at[slot, 1],
+            recv_sem=a2a_recv.at[slot, 1],
+            device_id=(to, d),
+            device_id_type=MESH,
+        )
+
+    def gather_start(slot):
+        def send(peer):
+            second_copy(
+                slot, mixed_out.at[slot, peer], mixed_in.at[slot, slot_here], peer
             ).start()
 
-        for zt in spread:
-            peers_of(zt, send, zt is z)
-        target[slot, me] = source[slot, me]
+        for zt in all_order:
+            peers_of(zt, send, True)
+        mixed_in[slot, slot_here] = mixed_out[slot, me]
+
+    def gather_wait(slot):
+        @pl.when(mid)
+        def _():
+            span = mixed_out.at[slot, pl.ds(0, crops - 1)]
+            second_copy(slot, span, span, me).wait_send()
+            span = mixed_in.at[slot, pl.ds(0, 31)]
+            second_copy(slot, span, span, me).wait_recv()
+
+        @pl.when(jnp.logical_not(mid))
+        def _():
+            span = mixed_in.at[slot]
+            second_copy(slot, span, span, me).wait_recv()
+
+    def far_copy(source, target, to):
+        return pltpu.make_async_remote_copy(
+            src_ref=source,
+            dst_ref=target,
+            send_sem=far_sems.at[0],
+            recv_sem=far_sems.at[1],
+            device_id=(to, 3 - d),
+            device_id_type=MESH,
+        )
 
     def far_start():
         @pl.when(middle)
         def _():
             def send(peer):
-                pltpu.make_async_remote_copy(
-                    src_ref=mixed_out.at[0, peer],
-                    dst_ref=far_in.at[me],
-                    send_sem=far_sems.at[0],
-                    recv_sem=far_sems.at[1],
-                    device_id=(peer, 3 - d),
-                    device_id_type=MESH,
-                ).start()
-
-            for zt in spread[::-1]:
+                far_copy(mixed_out.at[0, peer], far_in.at[slot_here], peer).start()
+
+            for zt in far_order:
                 peers_of(zt, send, False)
 
     def far_wait():
         @pl.when(middle)
         def _():
-            pltpu.make_async_remote_copy(
-                src_ref=mixed_out.at[0],
-                dst_ref=far_in,
-                send_sem=far_sems.at[0],
-                recv_sem=far_sems.at[1],
-                device_id=(me, mate),
-                device_id_type=MESH,
-            ).wait()
+            @pl.when(mid)
+            def _():
+                far_copy(mixed_out.at[0], mixed_out.at[0], me).wait_send()
+
+            far_copy(far_in, far_in, me).wait_recv()
 
     def near_copy():
         return pltpu.make_async_remote_copy(
@@ -400,21 +482,9 @@
             device_id_type=MESH,
         )
 
-    def scatter_wait(slot, phase, source, target):
-        copy = pltpu.make_async_remote_copy(
-            src_ref=source.at[slot, pl.ds(0, crops - 1)],
-            dst_ref=target.at[slot, pl.ds(0, crops - 1)],
-            send_sem=a2a_send.at[slot, phase],
-            recv_sem=a2a_recv.at[slot, phase],
-            device_id=(me, mate),
-            device_id_type=MESH,
-        )
-        copy.wait()
-
     def joined(pieces):
-        whole = pieces.astype(F32)
         return jnp.concatenate(
-            [whole[0:32].reshape(ROWS, 128), whole[32:64].reshape(ROWS, 128)], axis=1
+            [pieces[0:16].reshape(ROWS, 128), pieces[16:32].reshape(ROWS, 128)], axis=1
         )
 
     def kernel_grad(l, x, first, g):
@@ -465,9 +535,12 @@
             for k, to in enumerate((mate, far, far_mate))
         ]
 
-    def reduce_pairs(l):
+    def pair_sum(l):
         pair_copy(l).wait()
         kg_pair[l] = (part[l, core] + kg_recv[l].astype(F32)).astype(BF16)
+
+    def reduce_pairs(l):
+        pair_sum(l)
         for copy in all_copies(l):
             copy.start()
 
@@ -476,6 +549,28 @@
             copy.wait()
         own = kg_pair[l].astype(F32) + kg_all[l, 1].astype(F32)
         other = kg_all[l, 0].astype(F32) + kg_all[l, 2].astype(F32)
+        store_grads(l, own, other)
+
+    def share_copy(l):
+        return pltpu.make_async_remote_copy(
+            src_ref=kg_sum.at[l - 1],
+            dst_ref=kg_shared.at[l - 1],
+            send_sem=share_sems.at[l - 1, 0],
+            recv_sem=share_sems.at[l - 1, 1],
+            device_id=(me, mate),
+            device_id_type=MESH,
+        )
+
+    def reduce_share(l):
+        all_copies(l)[1].wait()
+        kg_sum[l - 1] = kg_pair[l].astype(F32) + kg_all[l, 1].astype(F32)
+        share_copy(l).start()
+
+    def share_finish(l):
+        share_copy(l).wait()
+        store_grads(l, kg_sum[l - 1], kg_shared[l - 1])
+
+    def store_grads(l, own, other):
         for a in range(3):
             for c in range(3):
                 k = 3 * a + c
@@ -510,7 +605,7 @@
         (crops, 128),
     )
     turn.start()
-    pl.semaphore_wait(barrier, crops + 2 + (crops - 1) * lax.rem((d + 1) // 2, 2))
+    pl.semaphore_wait(barrier, 35 + 31 * mid_count + 63 * mid_count * middle_count)
 
     xv, g1 = ext.at[0], ext.at[1]
     xb, xs, g3, g2, cotr = (wide.at[k] for k in range(5))
@@ -518,7 +613,7 @@
     halo_start(0)
 
     def first_layer(ranges):
-        v = conv(xv, 0, ranges, True)
+        v = conv_ranges(xv, 0, ranges, True)
         s = logistic(v)
         hidden = v * s
         slope = s * (1.0 + v * (1.0 - s))
@@ -539,7 +634,7 @@
     halo_wait(0)
     first_layer(((1, 2), (4, 5)))
 
-    scatter_start(0, 0, pieces_out, pieces_in)
+    scatter_start(0)
     cot_low, cot_high = cot_copies()
 
     @pl.when(d > 0)
@@ -551,40 +646,58 @@
         cot_high.start()
 
     build(2, True, True)
-    scatter_wait(0, 0, pieces_out, pieces_in)
-
-    def blend(n, carry):
-        own = pieces_in[0, n].astype(F32)
-        other = pieces_in[0, partner[0, n]].astype(F32)
-        mixed_out[0, n] = (OWN_SHARE * own + PARTNER_SHARE * other).astype(BF16)
-        return carry
-
-    lax.fori_loop(0, crops, blend, 0, unroll=8)
-    far_start()
-    scatter_start(0, 1, mixed_out, mixed_in)
+    scatter_wait(0)
+
+    def mix(slot, other_of):
+        def step(n, carry):
+            own = pieces_in[slot, n].astype(F32)
+            other = pieces_in[slot, other_of(n)].astype(F32)
+            mixed_out[slot, n] = (OWN_SHARE * own + PARTNER_SHARE * other).astype(BF16)
+            return carry
+
+        lax.fori_loop(0, crops, step, 0, unroll=8)
+
+    @pl.when(mid)
+    def _():
+        mix(0, lambda n: partner[0, n])
+        gather_start(0)
+        far_start()
+
     build(1, False, True)
     build(0, False, True)
-    scatter_wait(0, 1, mixed_out, mixed_in)
+    gather_wait(0)
     near_copy().start()
-    xb[4 * LAYER : 8 * LAYER, :] = joined(mixed_in[0]).astype(BF16)
-
-    def second_layer(s, t):
-        v = conv(xb, 1, ((s, t),), True)
+    xb[4 * LAYER : 8 * LAYER, :] = joined(mixed_in[0])
+
+    def far_masked(values):
+        parts = []
+        for k in range(4):
+            piece = values[LAYER * k : LAYER * (k + 1)]
+            if k == 0:
+                keep = middle | (core == 1)
+            elif k == 3:
+                keep = middle | (core == 0)
+            else:
+                keep = middle
+            parts.append(jnp.where(keep, piece, 0.0))
+        return jnp.concatenate(parts, axis=0)
+
+    def second_layer(s, n, mask):
+        v = conv(xb, 1, s, n, True)
         gate = logistic(v)
-        xs[LAYER * s : LAYER * t, :] = masked(v * gate, s).astype(BF16)
-        slope2[LAYER * s : LAYER * t, :] = gate * (1.0 + v * (1.0 - gate))
-
-    second_layer(5, 7)
+        second = v * gate
+        rows = at_rows(s, n)
+        xs[rows, :] = (far_masked(second) if mask else second).astype(BF16)
+        slope2[rows, :] = gate * (1.0 + v * (1.0 - gate))
+
+    second_layer(5, 2, False)
     far_wait()
 
     @pl.when(middle)
     def _():
-        xb[pl.ds(pl.multiple_of(512 * core, 512), 256), :] = joined(far_in[...]).astype(BF16)
-
-    near_copy().wait()
-    xb[pl.ds(pl.multiple_of(512 * (1 - core), 512), 256), :] = joined(near_in[...]).astype(BF16)
-    second_layer(1, 5)
-    second_layer(7, 11)
+        xb[pl.ds(pl.multiple_of(512 * core, 512), 256), :] = joined(far_in[...])
+
+    second_layer(1 + 6 * core, 4, True)
 
     @pl.when(d > 0)
     def _():
@@ -596,58 +709,70 @@
         cot_high.wait_send()
         cot_low.wait_recv()
 
-    def third_layer(s, t):
-        v = conv(xs, 2, ((s, t),), True)
+    def third_layer(s, far_side):
+        v = conv(xs, 2, s, 4, True)
         gate = logistic(v)
         slope = gate * (1.0 + v * (1.0 - gate))
-        facing = cotr[LAYER * s : LAYER * t, :].astype(F32)
-        g3[LAYER * s : LAYER * t, :] = masked(facing * slope, s).astype(BF16)
-
-    third_layer(2, 6)
-    third_layer(6, 10)
-
-    def back_three(s, t):
-        g = conv(g3, 2, ((s, t),), False) * slope2[LAYER * s : LAYER * t, :]
-        g2[LAYER * s : LAYER * t, :] = masked(g, s).astype(BF16)
-
-    back_three(3, 6)
-    back_three(6, 9)
-    fill_pieces(1, conv(g2, 1, ((4, 8),), False), 0)
-    scatter_start(1, 0, pieces_out, pieces_in)
+        rows = at_rows(s, 4)
+        values = cotr[rows, :].astype(F32) * slope
+        if far_side:
+            parts = []
+            for k in range(4):
+                piece = values[LAYER * k : LAYER * (k + 1)]
+                keep = middle | ((core == 1) if k < 2 else (core == 0))
+                parts.append(jnp.where(keep, piece, 0.0))
+            values = jnp.concatenate(parts, axis=0)
+        g3[rows, :] = values.astype(BF16)
+
+    third_layer(2 + 4 * core, True)
+    near_copy().wait()
+    xb[pl.ds(pl.multiple_of(512 * (1 - core), 512), 256), :] = joined(near_in[...])
+    second_layer(7 - 6 * core, 4, False)
+    third_layer(6 - 4 * core, False)
+
+    def back_three(s, n):
+        g = conv(g3, 2, s, n, False) * slope2[LAYER * s : LAYER * (s + n), :]
+        g2[LAYER * s : LAYER * (s + n), :] = masked(g, s).astype(BF16)
+
+    back_three(3, 3)
+    back_three(6, 3)
+    fill_pieces(1, conv(g2, 1, 4, 4, False), 0)
+    scatter_start(1)
     kernel_grad(2, xs, 3, g3[4 * LAYER : 8 * LAYER, :].astype(F32))
     pair_copy(2).start()
     kernel_grad(1, xb, 3, g2[4 * LAYER : 8 * LAYER, :].astype(F32))
     pair_copy(1).start()
-    reduce_pairs(2)
-    scatter_wait(1, 0, pieces_out, pieces_in)
+    pair_sum(2)
+    all_copies(2)[1].start()
+    pair_sum(1)
+    all_copies(1)[1].start()
     turn.wait()
-
-    def blend_back(n, carry):
-        own = pieces_in[1, n].astype(F32)
-        other = pieces_in[1, inverse[n, 0]].astype(F32)
-        mixed_out[1, n] = (OWN_SHARE * own + PARTNER_SHARE * other).astype(BF16)
-        return carry
-
-    lax.fori_loop(0, crops, blend_back, 0, unroll=8)
-    scatter_start(1, 1, mixed_out, mixed_in)
-    reduce_pairs(1)
-    reduce_finish(2)
-    scatter_wait(1, 1, mixed_out, mixed_in)
-
-    g_one = (joined(mixed_in[1]) * slope1[...]).astype(BF16)
+    scatter_wait(1)
+
+    @pl.when(mid)
+    def _():
+        mix(1, lambda n: inverse[n, 0])
+        gather_start(1)
+
+    reduce_share(2)
+    reduce_share(1)
+    share_finish(2)
+    share_finish(1)
+    gather_wait(1)
+
+    g_one = (joined(mixed_in[1]).astype(F32) * slope1[...]).astype(BF16)
     g1[LAYER : 5 * LAYER, :] = g_one
     halo_start(1)
     kernel_grad(0, xv, 0, g_one.astype(F32))
     pair_copy(0).start()
-    g = conv(g1, 0, ((2, 4),), False)
+    g = conv(g1, 0, 2, 2, False)
     gvol[0, 1] = from_rows(g[0:LAYER]).astype(BF16)
     gvol[0, 2] = from_rows(g[LAYER:]).astype(BF16)
     reduce_pairs(0)
     halo_wait(1)
-    g = conv(g1, 0, ((1, 2), (4, 5)), False)
+    g = conv_ranges(g1, 0, ((1, 2), (4, 5)), False)
     gvol[0, 0] = from_rows(g[0:LAYER]).astype(BF16)
     gvol[0, 3] = from_rows(g[LAYER:]).astype(BF16)
-    reduce_finish(1)
     reduce_finish(0)
 
 
@@ -679,16 +804,18 @@
             pltpu.VMEM((256, 256), F32),
             pltpu.VMEM((768, 256), F32),
             pltpu.VMEM((3, 2, 9, 16, 128), F32),
-            pltpu.VMEM((2, crops, 8, 128), BF16),
-            pltpu.VMEM((2, crops, 8, 128), BF16),
-            pltpu.VMEM((2, crops, 8, 128), BF16),
-            pltpu.VMEM((2, crops, 8, 128), BF16),
-            pltpu.VMEM((crops, 8, 128), BF16),
-            pltpu.VMEM((crops, 8, 128), BF16),
+            pltpu.VMEM((2, 32, 16, 128), BF16),
+            pltpu.VMEM((2, crops, 16, 128), BF16),
+            pltpu.VMEM((2, crops, 16, 128), BF16),
+            pltpu.VMEM((2, 32, 16, 128), BF16),
+            pltpu.VMEM((32, 16, 128), BF16),
+            pltpu.VMEM((32, 16, 128), BF16),
             pltpu.VMEM((3, 9, 16, 128), BF16),
             pltpu.VMEM((3, 9, 16, 128), BF16),
             pltpu.VMEM((3, 9, 16, 128), BF16),
             pltpu.VMEM((3, 3, 9, 16, 128), BF16),
+            pltpu.VMEM((2, 9, 16, 128), F32),
+            pltpu.VMEM((2, 9, 16, 128), F32),
             dma((2, 2)),
             dma((2, 2)),
             dma((2,)),
@@ -700,6 +827,7 @@
             dma((3, 2)),
             dma((3, 3)),
             dma((3, 3)),
+            dma((2, 2)),
             dma((6,)),
         ],
         compiler_params=pltpu.CompilerParams(

time: 64.6 us -> 59.5 us (0.921)
  Pallas kernels: 62.5 us -> 57.4 us
    pallas_call x1, Pallas kernels: 62.5 us -> 57.4 us  [per_device(): pl.pallas_call(functools.partial(kernel, crops), out_shape=(jax.ShapeDtyp...]
where the time goes in v3:
time: 59.5 us; the launch traced here: 59.4 us
  Pallas kernels  57.4 us (96%)
  local copies, waits for them, and re-layouts  1.38 us (2%)
  between operations  0.64 us (1%)
    pallas_call x1, Pallas kernels, per_device(): pl.pallas_call(functools.partial(kernel, crops), out_shape=(jax.ShapeDtyp...  57.4 us
    unnamed x2, local copies, waits for them, and re-layouts  1.38 us

profile of v3, /device:TPU:1, one launch (start us, length us, event | category | flops | bytes accessed | tf_op | source)
XLA Modules:
  0.0 59.4 jit_solution(5556572678916621393)
XLA Ops:
  0.6 57.4 %shard_map.59 = (bf16[1,4,8,2048]{3,2,1,0:T(8,128)(2,1)S(1)}, f32[81,8,128]{2,1,0:T(8,128)S(1)}) custom-call(s32[1,64]{1,0:T(1,128)} %bitcast.3, bf16[1,4,8,2048]{3,2,1,0:T(8,128)(2,1)} %vol_hbm.1, bf16[1,4,8,2048]{3,2,1,0:T(8,128)(2,1)} %cot_hbm.1, bf16[3,27,1024]{2,1,0:T(8,128)(2,1)} %kern_hbm.1), custom_call_target="tpu_custom_call" | custom-call | tf_op jit(solution)/shard_map/pallas_call | solution.py:783
  58.0 0.7 %copy.10 = bf16[1,4,8,2048]{3,2,1,0:T(8,128)(2,1)} copy(bf16[1,4,8,2048]{3,2,1,0:T(8,128)(2,1)S(1)} %get-tuple-element.12) | data formatting | bytes 262144
  58.7 0.7 %copy.11 = f32[1,3,27,1024]{3,0,2,1:T(1,128)} copy(f32[1,3,27,1024]{3,0,2,1:T(1,128)S(1)} %bitcast.2) | data formatting | bytes 663552

commit v4 on v3

--- a/solution.py
+++ b/solution.py
@@ -143,7 +143,6 @@
     mid = (z == 1) | (z == 2)
     middle = (d == 1) | (d == 2)
     mid_count = lax.rem((z + 1) // 2, 2)
-    middle_count = lax.rem((d + 1) // 2, 2)
     slot_here = me - 16
     ys = [lax.rem(me + 2 + k, 4) for k in range(4)]
     xs_far = me // 4 + 2
@@ -187,11 +186,6 @@
         pl.semaphore_signal(
             barrier, inc=1, device_id=(me, lax.rem(d + k, 4)), device_id_type=MESH
         )
-
-    @pl.when(middle)
-    def _():
-        for zt in mid_order:
-            peers_of(zt, greet(3 - d), True)
 
     loads[0].wait()
     for layer in range(4):
@@ -491,6 +485,7 @@
         stacked = jnp.concatenate(
             [from_right(g).astype(BF16), g.astype(BF16), from_left(g).astype(BF16)], axis=1
         )
+        totals = []
         for a in range(3):
             u = x[LAYER * (first + a) : LAYER * (first + a) + ROWS, :]
             for c in range(3):
@@ -508,8 +503,14 @@
                 total = (
                     g0 + pltpu.roll(g1, 96, 1) + pltpu.roll(g2, 64, 1) + pltpu.roll(g3, 32, 1)
                 )
-                part[l, 0, 3 * a + c] = total[0:16]
-                part[l, 1, 3 * a + c] = total[16:32]
+                totals.append(total)
+        for k in range(6):
+            extra = pltpu.roll(totals[6 + k // 3], 32 * (3 - k % 3), 1)
+            packed = jnp.where(blk32 == 3, extra, totals[k])
+            part[l, 0, k] = packed[0:16]
+            part[l, 1, k] = packed[16:32]
+        part[l, 0, 6] = totals[8][0:16]
+        part[l, 1, 6] = totals[8][16:32]
         kg_send[l] = part[l, 1 - core].astype(BF16)
 
     def pair_copy(l):
@@ -571,16 +572,26 @@
         store_grads(l, kg_sum[l - 1], kg_shared[l - 1])
 
     def store_grads(l, own, other):
+        tiles = [
+            jnp.concatenate(
+                [
+                    jnp.where(core == 0, own[k], other[k]),
+                    jnp.where(core == 0, other[k], own[k]),
+                ],
+                axis=0,
+            )
+            for k in range(7)
+        ]
+        terms = tiles[:6]
+        for k in (0, 3):
+            term = pltpu.roll(tiles[k], 32, 1)
+            for m in (1, 2):
+                term = jnp.where(blk32 == m, pltpu.roll(tiles[k + m], 32 * (m + 1), 1), term)
+            terms.append(term)
+        terms.append(tiles[6])
         for a in range(3):
             for c in range(3):
-                k = 3 * a + c
-                x = jnp.concatenate(
-                    [
-                        jnp.where(core == 0, own[k], other[k]),
-                        jnp.where(core == 0, other[k], own[k]),
-                    ],
-                    axis=0,
-                )
+                x = terms[3 * a + c]
                 turned = [x] + [pltpu.roll(x, 32 * m, 1) for m in (1, 2, 3)]
                 for b in range(3):
                     z = jnp.zeros_like(x)
@@ -605,7 +616,7 @@
         (crops, 128),
     )
     turn.start()
-    pl.semaphore_wait(barrier, 35 + 31 * mid_count + 63 * mid_count * middle_count)
+    pl.semaphore_wait(barrier, 35 + 31 * mid_count)
 
     xv, g1 = ext.at[0], ext.at[1]
     xb, xs, g3, g2, cotr = (wide.at[k] for k in range(5))
@@ -660,8 +671,8 @@
     @pl.when(mid)
     def _():
         mix(0, lambda n: partner[0, n])
+        far_start()
         gather_start(0)
-        far_start()
 
     build(1, False, True)
     build(0, False, True)
@@ -803,19 +814,19 @@
             pltpu.VMEM((5, 768, 256), BF16),
             pltpu.VMEM((256, 256), F32),
             pltpu.VMEM((768, 256), F32),
-            pltpu.VMEM((3, 2, 9, 16, 128), F32),
+            pltpu.VMEM((3, 2, 7, 16, 128), F32),
             pltpu.VMEM((2, 32, 16, 128), BF16),
             pltpu.VMEM((2, crops, 16, 128), BF16),
             pltpu.VMEM((2, crops, 16, 128), BF16),
             pltpu.VMEM((2, 32, 16, 128), BF16),
             pltpu.VMEM((32, 16, 128), BF16),
             pltpu.VMEM((32, 16, 128), BF16),
-            pltpu.VMEM((3, 9, 16, 128), BF16),
-            pltpu.VMEM((3, 9, 16, 128), BF16),
-            pltpu.VMEM((3, 9, 16, 128), BF16),
-            pltpu.VMEM((3, 3, 9, 16, 128), BF16),
-            pltpu.VMEM((2, 9, 16, 128), F32),
-            pltpu.VMEM((2, 9, 16, 128), F32),
+            pltpu.VMEM((3, 7, 16, 128), BF16),
+            pltpu.VMEM((3, 7, 16, 128), BF16),
+            pltpu.VMEM((3, 7, 16, 128), BF16),
+            pltpu.VMEM((3, 3, 7, 16, 128), BF16),
+            pltpu.VMEM((2, 7, 16, 128), F32),
+            pltpu.VMEM((2, 7, 16, 128), F32),
             dma((2, 2)),
             dma((2, 2)),
             dma((2,)),

time: 59.5 us -> 59.6 us (level)
  no operation moved by 1% of the time
where the time goes in v4:
time: 59.6 us; the launch traced here: 59.5 us
  Pallas kernels  57.5 us (96%)
  local copies, waits for them, and re-layouts  1.38 us (2%)
  between operations  0.64 us (1%)
    pallas_call x1, Pallas kernels, per_device(): pl.pallas_call(functools.partial(kernel, crops), out_shape=(jax.ShapeDtyp...  57.5 us
    unnamed x2, local copies, waits for them, and re-layouts  1.38 us

profile of v4, /device:TPU:1, one launch (start us, length us, event | category | flops | bytes accessed | tf_op | source)
XLA Modules:
  0.0 59.5 jit_solution(15735295576565055799)
XLA Ops:
  0.6 57.5 %shard_map.59 = (bf16[1,4,8,2048]{3,2,1,0:T(8,128)(2,1)S(1)}, f32[81,8,128]{2,1,0:T(8,128)S(1)}) custom-call(s32[1,64]{1,0:T(1,128)} %bitcast.3, bf16[1,4,8,2048]{3,2,1,0:T(8,128)(2,1)} %vol_hbm.1, bf16[1,4,8,2048]{3,2,1,0:T(8,128)(2,1)} %cot_hbm.1, bf16[3,27,1024]{2,1,0:T(8,128)(2,1)} %kern_hbm.1), custom_call_target="tpu_custom_call" | custom-call | tf_op jit(solution)/shard_map/pallas_call | solution.py:794
  58.1 0.7 %copy.10 = bf16[1,4,8,2048]{3,2,1,0:T(8,128)(2,1)} copy(bf16[1,4,8,2048]{3,2,1,0:T(8,128)(2,1)S(1)} %get-tuple-element.12) | data formatting | bytes 262144
  58.8 0.7 %copy.11 = f32[1,3,27,1024]{3,0,2,1:T(1,128)} copy(f32[1,3,27,1024]{3,0,2,1:T(1,128)S(1)} %bitcast.2) | data formatting | bytes 663552

commit v5 on v4

--- a/solution.py
+++ b/solution.py
@@ -116,6 +116,7 @@
     all_recv,
     share_sems,
     load_sems,
+    levels,
 ):
     loads = [
         pltpu.make_async_copy(source, target, load_sems.at[k])
@@ -147,18 +148,19 @@
     ys = [lax.rem(me + 2 + k, 4) for k in range(4)]
     xs_far = me // 4 + 2
 
-    def peers_of(zt, send, skip_own):
+    def peers_of(zts, send, skip_own):
         @pl.loop(0, 4)
         def _(k):
-            row = 16 * zt + 4 * lax.rem(xs_far + k, 4)
+            row = 4 * lax.rem(xs_far + k, 4)
             for at, y in enumerate(ys):
-                if skip_own and at == 2:
-
-                    @pl.when((k != 2) | (zt != z))
-                    def _():
-                        send(row + y)
-                else:
-                    send(row + y)
+                for zt in zts:
+                    if skip_own and at == 2:
+
+                        @pl.when((k != 2) | (zt != z))
+                        def _():
+                            send(16 * zt + row + y)
+                    else:
+                        send(16 * zt + row + y)
 
     mids_first = 1 + mid_count * (2 - z) + (1 - mid_count) * (1 - z // 3)
     mid_order = (mids_first, 3 - mids_first)
@@ -168,24 +170,21 @@
 
     barrier = pltpu.get_barrier_semaphore()
 
-    def greet(depth):
-        def signal(peer):
-            pl.semaphore_signal(barrier, inc=1, device_id=(peer, depth), device_id_type=MESH)
-
-        return signal
-
-    for zt in mid_order:
-        peers_of(zt, greet(d), True)
-
-    @pl.when(mid)
-    def _():
-        for zt in (0, 3):
-            peers_of(zt, greet(d), False)
-
-    for k in (1, 2, 3):
+    x_line = [16 * z + 4 * lax.rem(me // 4 + k, 4) + lax.rem(me, 4) for k in (1, 2, 3)]
+    y_line = [4 * (me // 4) + lax.rem(me + k, 4) for k in (1, 2, 3)]
+    z_line = [16 * lax.rem(z + k, 4) + lax.rem(me, 16) for k in (2, 1, 3)]
+    for k in (2, 3, 1):
         pl.semaphore_signal(
             barrier, inc=1, device_id=(me, lax.rem(d + k, 4)), device_id_type=MESH
         )
+    for peer in z_line + x_line + y_line:
+        pl.semaphore_signal(barrier, inc=1, device_id=(peer, d), device_id_type=MESH)
+
+    def tell(level, peers):
+        for peer in peers:
+            pl.semaphore_signal(
+                levels.at[level], inc=1, device_id=(peer, d), device_id_type=MESH
+            )
 
     loads[0].wait()
     for layer in range(4):
@@ -205,9 +204,6 @@
             ext[k, 5 * LAYER : 6 * LAYER, :] = jnp.zeros((LAYER, LANES), BF16)
         wide[0, 8 * LAYER : 12 * LAYER, :] = jnp.zeros((4 * LAYER, LANES), BF16)
 
-    loads[1].wait()
-    for l in range(3):
-        kf[l] = kern[l].astype(F32)
 
     sub = lax.broadcasted_iota(jnp.int32, (8, 128), 0)
     blk8 = lax.broadcasted_iota(jnp.int32, (8, 128), 1) // 32
@@ -385,8 +381,7 @@
         def send(peer):
             first_copy(slot, pieces_out.at[slot, peer - 16], pieces_in.at[slot, me], peer).start()
 
-        for zt in mid_order:
-            peers_of(zt, send, True)
+        peers_of(mid_order, send, True)
 
         @pl.when(mid)
         def _():
@@ -421,8 +416,7 @@
                 slot, mixed_out.at[slot, peer], mixed_in.at[slot, slot_here], peer
             ).start()
 
-        for zt in all_order:
-            peers_of(zt, send, True)
+        peers_of(all_order, send, True)
         mixed_in[slot, slot_here] = mixed_out[slot, me]
 
     def gather_wait(slot):
@@ -454,8 +448,7 @@
             def send(peer):
                 far_copy(mixed_out.at[0, peer], far_in.at[slot_here], peer).start()
 
-            for zt in far_order:
-                peers_of(zt, send, False)
+            peers_of(far_order, send, False)
 
     def far_wait():
         @pl.when(middle)
@@ -605,6 +598,12 @@
                         kg[t, 2 * r : 2 * r + 1, :] = z[r, 0:1, :]
                         kg[t, 2 * r + 1 : 2 * r + 2, :] = z[r, 4:5, :]
 
+    pl.semaphore_wait(barrier, 12)
+    halo_start(0)
+    tell(0, x_line)
+    loads[1].wait()
+    for l in range(3):
+        kf[l] = kern[l].astype(F32)
     build(0, True, False)
     for load in loads[2:4]:
         load.wait()
@@ -616,12 +615,10 @@
         (crops, 128),
     )
     turn.start()
-    pl.semaphore_wait(barrier, 35 + 31 * mid_count)
 
     xv, g1 = ext.at[0], ext.at[1]
     xb, xs, g3, g2, cotr = (wide.at[k] for k in range(5))
 
-    halo_start(0)
 
     def first_layer(ranges):
         v = conv_ranges(xv, 0, ranges, True)
@@ -641,10 +638,13 @@
         cotr[LAYER * (layer + 4) : LAYER * (layer + 5), :] = to_rows(
             cot[0, layer].astype(F32)
         ).astype(BF16)
+    pl.semaphore_wait(levels.at[0], 3)
+    tell(1, z_line)
     build(1, True, False)
     halo_wait(0)
     first_layer(((1, 2), (4, 5)))
 
+    pl.semaphore_wait(levels.at[1], 3)
     scatter_start(0)
     cot_low, cot_high = cot_copies()
 
@@ -785,6 +785,17 @@
     gvol[0, 0] = from_rows(g[0:LAYER]).astype(BF16)
     gvol[0, 3] = from_rows(g[LAYER:]).astype(BF16)
     reduce_finish(0)
+
+
+def write_out(gvol, kg, gvol_out, kg_out, sems):
+    copies = (
+        pltpu.make_async_copy(gvol, gvol_out, sems.at[0]),
+        pltpu.make_async_copy(kg, kg_out, sems.at[1]),
+    )
+    for copy in copies:
+        copy.start()
+    for copy in copies:
+        copy.wait()
 
 
 def per_device(crops, volume, kernels, partner, cotangent):
@@ -840,11 +851,23 @@
             dma((3, 3)),
             dma((2, 2)),
             dma((6,)),
+            pltpu.SemaphoreType.REGULAR((2,)),
         ],
         compiler_params=pltpu.CompilerParams(
             collective_id=0, has_side_effects=True, vmem_limit_bytes=48 * 1024 * 1024
         ),
     )(*(pltpu.with_memory_space_constraint(x, pltpu.HBM) for x in (partner[None, :], volume, cotangent, kernels)))
+    grad_volume, kg = pl.pallas_call(
+        write_out,
+        out_shape=(
+            jax.ShapeDtypeStruct((1, 4, 8, 2048), BF16),
+            jax.ShapeDtypeStruct((81, 8, 128), F32),
+        ),
+        in_specs=[vmem, vmem],
+        out_specs=(hbm, hbm),
+        scratch_shapes=[dma((2,))],
+        compiler_params=pltpu.CompilerParams(vmem_limit_bytes=1024 * 1024),
+    )(grad_volume, kg)
     return grad_volume, kg.reshape(1, 3, 27, CH * CH)
 
 

time: 59.6 us -> 57.9 us (0.971); the launches traced: 59.5 us -> 57.2 us
  local copies, waits for them, and re-layouts: 1.38 us -> 0 us
  Pallas kernels: 57.5 us -> 56.5 us
    pallas_call x1, Pallas kernels: 57.5 us -> 55.8 us  [per_device(): pl.pallas_call(functools.partial(kernel, crops), out_shape=(jax.ShapeDtyp...]
    unnamed x2 -> x0, local copies, waits for them, and re-layouts: 1.38 us -> none
    pallas_call x0 -> x1, Pallas kernels: none -> 0.79 us  [per_device(): pl.pallas_call(write_out, out_shape=(jax.ShapeDtypeStruct((1, 4, 8, 2048)...]
where the time goes in v5:
time: 57.9 us; the launch traced here: 57.2 us
  Pallas kernels  56.5 us (98%)
  between operations  0.64 us (1%)
    pallas_call x1, Pallas kernels, per_device(): pl.pallas_call(functools.partial(kernel, crops), out_shape=(jax.ShapeDtyp...  55.8 us

profile of v5, /device:TPU:1, one launch (start us, length us, event | category | flops | bytes accessed | tf_op | source)
XLA Modules:
  0.0 57.2 jit_solution(15685764669233701671)
XLA Ops:
  0.6 55.8 %shard_map.59 = (bf16[1,4,8,2048]{3,2,1,0:T(8,128)(2,1)S(1)}, f32[81,8,128]{2,1,0:T(8,128)S(1)}) custom-call(s32[1,64]{1,0:T(1,128)} %bitcast.2, bf16[1,4,8,2048]{3,2,1,0:T(8,128)(2,1)} %vol_hbm.1, bf16[1,4,8,2048]{3,2,1,0:T(8,128)(2,1)} %cot_hbm.1, bf16[3,27,1024]{2,1,0:T(8,128)(2,1)} %kern_hbm.1), custom_call_target="tpu_custom_call" | custom-call | tf_op jit(solution)/shard_map/pallas_call | solution.py:805
  56.4 0.8 %shard_map.60 = (bf16[1,4,8,2048]{3,2,1,0:T(8,128)(2,1)}, f32[81,8,128]{2,1,0:T(8,128)}) custom-call(bf16[1,4,8,2048]{3,2,1,0:T(8,128)(2,1)S(1)} %get-tuple-element.6.gvol, f32[81,8,128]{2,1,0:T(8,128)S(1)} %get-tuple-element.7.kg), custom_call_target="tpu_custom_call" | custom-call | tf_op jit(solution)/shard_map/pallas_call | solution.py:860

commit v6 on v5

--- a/solution.py
+++ b/solution.py
@@ -638,6 +638,16 @@
         cotr[LAYER * (layer + 4) : LAYER * (layer + 5), :] = to_rows(
             cot[0, layer].astype(F32)
         ).astype(BF16)
+    cot_low, cot_high = cot_copies()
+
+    @pl.when(d > 0)
+    def _():
+        cot_low.start()
+
+    @pl.when(d < 3)
+    def _():
+        cot_high.start()
+
     pl.semaphore_wait(levels.at[0], 3)
     tell(1, z_line)
     build(1, True, False)
@@ -646,16 +656,6 @@
 
     pl.semaphore_wait(levels.at[1], 3)
     scatter_start(0)
-    cot_low, cot_high = cot_copies()
-
-    @pl.when(d > 0)
-    def _():
-        cot_low.start()
-
-    @pl.when(d < 3)
-    def _():
-        cot_high.start()
-
     build(2, True, True)
     scatter_wait(0)
 
@@ -753,22 +753,18 @@
     pair_copy(2).start()
     kernel_grad(1, xb, 3, g2[4 * LAYER : 8 * LAYER, :].astype(F32))
     pair_copy(1).start()
+    turn.wait()
+    scatter_wait(1)
+
+    @pl.when(mid)
+    def _():
+        mix(1, lambda n: inverse[n, 0])
+        gather_start(1)
+
     pair_sum(2)
     all_copies(2)[1].start()
     pair_sum(1)
     all_copies(1)[1].start()
-    turn.wait()
-    scatter_wait(1)
-
-    @pl.when(mid)
-    def _():
-        mix(1, lambda n: inverse[n, 0])
-        gather_start(1)
-
-    reduce_share(2)
-    reduce_share(1)
-    share_finish(2)
-    share_finish(1)
     gather_wait(1)
 
     g_one = (joined(mixed_in[1]).astype(F32) * slope1[...]).astype(BF16)
@@ -776,6 +772,8 @@
     halo_start(1)
     kernel_grad(0, xv, 0, g_one.astype(F32))
     pair_copy(0).start()
+    reduce_share(2)
+    reduce_share(1)
     g = conv(g1, 0, 2, 2, False)
     gvol[0, 1] = from_rows(g[0:LAYER]).astype(BF16)
     gvol[0, 2] = from_rows(g[LAYER:]).astype(BF16)
@@ -784,6 +782,8 @@
     g = conv_ranges(g1, 0, ((1, 2), (4, 5)), False)
     gvol[0, 0] = from_rows(g[0:LAYER]).astype(BF16)
     gvol[0, 3] = from_rows(g[LAYER:]).astype(BF16)
+    share_finish(2)
+    share_finish(1)
     reduce_finish(0)
 
 

time: 57.9 us -> 57 us (0.984); the launches traced: 57.2 us -> 56.9 us
  no operation moved by 1% of the time
where the time goes in v6:
time: 57 us; the launch traced here: 56.9 us
  Pallas kernels  56.2 us (99%)
  between operations  0.64 us (1%)
    pallas_call x1, Pallas kernels, per_device(): pl.pallas_call(functools.partial(kernel, crops), out_shape=(jax.ShapeDtyp...  55.5 us

profile of v6, /device:TPU:1, one launch (start us, length us, event | category | flops | bytes accessed | tf_op | source)
XLA Modules:
  0.0 56.9 jit_solution(11026449017164005257)
XLA Ops:
  0.6 55.5 %shard_map.59 = (bf16[1,4,8,2048]{3,2,1,0:T(8,128)(2,1)S(1)}, f32[81,8,128]{2,1,0:T(8,128)S(1)}) custom-call(s32[1,64]{1,0:T(1,128)} %bitcast.2, bf16[1,4,8,2048]{3,2,1,0:T(8,128)(2,1)} %vol_hbm.1, bf16[1,4,8,2048]{3,2,1,0:T(8,128)(2,1)} %cot_hbm.1, bf16[3,27,1024]{2,1,0:T(8,128)(2,1)} %kern_hbm.1), custom_call_target="tpu_custom_call" | custom-call | tf_op jit(solution)/shard_map/pallas_call | solution.py:805
  56.1 0.8 %shard_map.60 = (bf16[1,4,8,2048]{3,2,1,0:T(8,128)(2,1)}, f32[81,8,128]{2,1,0:T(8,128)}) custom-call(bf16[1,4,8,2048]{3,2,1,0:T(8,128)(2,1)S(1)} %get-tuple-element.6.gvol, f32[81,8,128]{2,1,0:T(8,128)S(1)} %get-tuple-element.7.kg), custom_call_target="tpu_custom_call" | custom-call | tf_op jit(solution)/shard_map/pallas_call | solution.py:860

commit v7 on v6

--- a/solution.py
+++ b/solution.py
@@ -680,14 +680,20 @@
     near_copy().start()
     xb[4 * LAYER : 8 * LAYER, :] = joined(mixed_in[0])
 
+    upper = d // 2
+
+    def near_store():
+        near_copy().wait()
+        xb[pl.ds(pl.multiple_of(512 * (1 - core), 512), 256), :] = joined(near_in[...])
+
     def far_masked(values):
         parts = []
         for k in range(4):
             piece = values[LAYER * k : LAYER * (k + 1)]
             if k == 0:
-                keep = middle | (core == 1)
+                keep = middle | (upper == 1)
             elif k == 3:
-                keep = middle | (core == 0)
+                keep = middle | (upper == 0)
             else:
                 keep = middle
             parts.append(jnp.where(keep, piece, 0.0))
@@ -702,13 +708,12 @@
         slope2[rows, :] = gate * (1.0 + v * (1.0 - gate))
 
     second_layer(5, 2, False)
-    far_wait()
 
     @pl.when(middle)
     def _():
-        xb[pl.ds(pl.multiple_of(512 * core, 512), 256), :] = joined(far_in[...])
-
-    second_layer(1 + 6 * core, 4, True)
+        near_store()
+
+    second_layer(1 + 6 * upper, 4, True)
 
     @pl.when(d > 0)
     def _():
@@ -730,16 +735,24 @@
             parts = []
             for k in range(4):
                 piece = values[LAYER * k : LAYER * (k + 1)]
-                keep = middle | ((core == 1) if k < 2 else (core == 0))
+                keep = middle | ((upper == 1) if k < 2 else (upper == 0))
                 parts.append(jnp.where(keep, piece, 0.0))
             values = jnp.concatenate(parts, axis=0)
         g3[rows, :] = values.astype(BF16)
 
-    third_layer(2 + 4 * core, True)
-    near_copy().wait()
-    xb[pl.ds(pl.multiple_of(512 * (1 - core), 512), 256), :] = joined(near_in[...])
-    second_layer(7 - 6 * core, 4, False)
-    third_layer(6 - 4 * core, False)
+    third_layer(2 + 4 * upper, True)
+    far_wait()
+
+    @pl.when(middle)
+    def _():
+        xb[pl.ds(pl.multiple_of(512 * core, 512), 256), :] = joined(far_in[...])
+
+    @pl.when(jnp.logical_not(middle))
+    def _():
+        near_store()
+
+    second_layer(7 - 6 * upper, 4, False)
+    third_layer(6 - 4 * upper, False)
 
     def back_three(s, n):
         g = conv(g3, 2, s, n, False) * slope2[LAYER * s : LAYER * (s + n), :]

time: 57 us -> 57.1 us (level)
  no operation moved by 1% of the time
where the time goes in v7:
time: 57.1 us; the launch traced here: 56.8 us
  Pallas kernels  56.2 us (98%)
  between operations  0.64 us (1%)
    pallas_call x1, Pallas kernels, per_device(): pl.pallas_call(functools.partial(kernel, crops), out_shape=(jax.ShapeDtyp...  55.4 us

profile of v7, /device:TPU:1, one launch (start us, length us, event | category | flops | bytes accessed | tf_op | source)
XLA Modules:
  0.0 56.8 jit_solution(13869123142923057560)
XLA Ops:
  0.6 55.4 %shard_map.59 = (bf16[1,4,8,2048]{3,2,1,0:T(8,128)(2,1)S(1)}, f32[81,8,128]{2,1,0:T(8,128)S(1)}) custom-call(s32[1,64]{1,0:T(1,128)} %bitcast.2, bf16[1,4,8,2048]{3,2,1,0:T(8,128)(2,1)} %vol_hbm.1, bf16[1,4,8,2048]{3,2,1,0:T(8,128)(2,1)} %cot_hbm.1, bf16[3,27,1024]{2,1,0:T(8,128)(2,1)} %kern_hbm.1), custom_call_target="tpu_custom_call" | custom-call | tf_op jit(solution)/shard_map/pallas_call | solution.py:818
  56.0 0.8 %shard_map.60 = (bf16[1,4,8,2048]{3,2,1,0:T(8,128)(2,1)}, f32[81,8,128]{2,1,0:T(8,128)}) custom-call(bf16[1,4,8,2048]{3,2,1,0:T(8,128)(2,1)S(1)} %get-tuple-element.6.gvol, f32[81,8,128]{2,1,0:T(8,128)S(1)} %get-tuple-element.7.kg), custom_call_target="tpu_custom_call" | custom-call | tf_op jit(solution)/shard_map/pallas_call | solution.py:873

commit v8 on v7

--- a/solution.py
+++ b/solution.py
@@ -671,8 +671,8 @@
     @pl.when(mid)
     def _():
         mix(0, lambda n: partner[0, n])
+        gather_start(0)
         far_start()
-        gather_start(0)
 
     build(1, False, True)
     build(0, False, True)

time: 57.1 us -> 56.6 us (level)
  no operation moved by 1% of the time
where the time goes in v8:
time: 56.6 us; the launch traced here: 56.5 us
  Pallas kernels  55.9 us (99%)
  between operations  0.64 us (1%)
    pallas_call x1, Pallas kernels, per_device(): pl.pallas_call(functools.partial(kernel, crops), out_shape=(jax.ShapeDtyp...  55.1 us

profile of v8, /device:TPU:1, one launch (start us, length us, event | category | flops | bytes accessed | tf_op | source)
XLA Modules:
  0.0 56.5 jit_solution(16195596805635715870)
XLA Ops:
  0.6 55.1 %shard_map.59 = (bf16[1,4,8,2048]{3,2,1,0:T(8,128)(2,1)S(1)}, f32[81,8,128]{2,1,0:T(8,128)S(1)}) custom-call(s32[1,64]{1,0:T(1,128)} %bitcast.2, bf16[1,4,8,2048]{3,2,1,0:T(8,128)(2,1)} %vol_hbm.1, bf16[1,4,8,2048]{3,2,1,0:T(8,128)(2,1)} %cot_hbm.1, bf16[3,27,1024]{2,1,0:T(8,128)(2,1)} %kern_hbm.1), custom_call_target="tpu_custom_call" | custom-call | tf_op jit(solution)/shard_map/pallas_call | solution.py:818
  55.7 0.8 %shard_map.60 = (bf16[1,4,8,2048]{3,2,1,0:T(8,128)(2,1)}, f32[81,8,128]{2,1,0:T(8,128)}) custom-call(bf16[1,4,8,2048]{3,2,1,0:T(8,128)(2,1)S(1)} %get-tuple-element.6.gvol, f32[81,8,128]{2,1,0:T(8,128)S(1)} %get-tuple-element.7.kg), custom_call_target="tpu_custom_call" | custom-call | tf_op jit(solution)/shard_map/pallas_call | solution.py:873

commit v9 on v8

--- a/solution.py
+++ b/solution.py
@@ -117,6 +117,7 @@
     share_sems,
     load_sems,
     levels,
+    turned_xv,
 ):
     loads = [
         pltpu.make_async_copy(source, target, load_sems.at[k])
@@ -482,9 +483,11 @@
         for a in range(3):
             u = x[LAYER * (first + a) : LAYER * (first + a) + ROWS, :]
             for c in range(3):
-                r = lax.dot_general(
-                    u, stacked[:, 256 * c : 256 * c + 256], TN, preferred_element_type=F32
-                )
+                g_c = stacked[:, 256 * c : 256 * c + 256]
+                if l == 0:
+                    r = jnp.dot(turned_xv[a], g_c, preferred_element_type=F32)
+                else:
+                    r = lax.dot_general(u, g_c, TN, preferred_element_type=F32)
 
                 def at(hp, j):
                     return r[32 * hp : 32 * hp + 32, 128 * j : 128 * j + 128]
@@ -676,6 +679,8 @@
 
     build(1, False, True)
     build(0, False, True)
+    for a in range(3):
+        turned_xv[a] = xv[LAYER * a : LAYER * a + ROWS, :].astype(F32).T.astype(BF16)
     gather_wait(0)
     near_copy().start()
     xb[4 * LAYER : 8 * LAYER, :] = joined(mixed_in[0])
@@ -865,6 +870,7 @@
             dma((2, 2)),
             dma((6,)),
             pltpu.SemaphoreType.REGULAR((2,)),
+            pltpu.VMEM((3, 256, 256), BF16),
         ],
         compiler_params=pltpu.CompilerParams(
             collective_id=0, has_side_effects=True, vmem_limit_bytes=48 * 1024 * 1024

time: 56.6 us -> 56.5 us (level)
  no operation moved by 1% of the time
where the time goes in v9:
time: 56.5 us; the launch traced here: 56.4 us
  Pallas kernels  55.8 us (99%)
  between operations  0.64 us (1%)
    pallas_call x1, Pallas kernels, per_device(): pl.pallas_call(functools.partial(kernel, crops), out_shape=(jax.ShapeDtyp...  55 us

profile of v9, /device:TPU:1, one launch (start us, length us, event | category | flops | bytes accessed | tf_op | source)
XLA Modules:
  0.0 56.4 jit_solution(10354671721068745494)
XLA Ops:
  0.6 55.0 %shard_map.59 = (bf16[1,4,8,2048]{3,2,1,0:T(8,128)(2,1)S(1)}, f32[81,8,128]{2,1,0:T(8,128)S(1)}) custom-call(s32[1,64]{1,0:T(1,128)} %bitcast.2, bf16[1,4,8,2048]{3,2,1,0:T(8,128)(2,1)} %vol_hbm.1, bf16[1,4,8,2048]{3,2,1,0:T(8,128)(2,1)} %cot_hbm.1, bf16[3,27,1024]{2,1,0:T(8,128)(2,1)} %kern_hbm.1), custom_call_target="tpu_custom_call" | custom-call | tf_op jit(solution)/shard_map/pallas_call | solution.py:823
  55.7 0.8 %shard_map.60 = (bf16[1,4,8,2048]{3,2,1,0:T(8,128)(2,1)}, f32[81,8,128]{2,1,0:T(8,128)}) custom-call(bf16[1,4,8,2048]{3,2,1,0:T(8,128)(2,1)S(1)} %get-tuple-element.6.gvol, f32[81,8,128]{2,1,0:T(8,128)S(1)} %get-tuple-element.7.kg), custom_call_target="tpu_custom_call" | custom-call | tf_op jit(solution)/shard_map/pallas_call | solution.py:879
